TPU v7x, 512 devices: a whole 4x4x16 slice. The times are simulated.
512 devices in a mesh: dp: 32 (over z, core), cent: 16 (over x, y).
Axes of the slice: x: 4, y: 4, z: 16, core: 2. Of those that a mesh axis runs over, the one named last changes fastest.
Arguments:
- embeddings: bfloat16 [262144, 1024], P(('dp', 'cent')), may hold values from -44.5 to 53.875
- centroids: float32 [131072, 1024], P(('dp', 'cent')), may hold values from -3 to 5
- candidates: int32 [1024, 8], P(('dp', 'cent')), may hold values from 0 to 15, all different within a row; in each aligned block of 32 rows (0 to 31, 32 to 63, ...) at most 24 rows name the same one
Outputs:
- new_centroids: float32 [131072, 1024], P(('dp', 'cent'))
- log_norm: float32 [262144], P(('dp', 'cent'))
- objective: float32 [], replicated
Inputs may be any that keep to these rules, and one draw needn't show every extreme that they name: `candidates`: the 8 entries of a row block are different. Among the row blocks of one coarse group (aligned runs of 32 row blocks), no centroid block is named more than 24 times, and some centroid block is named exactly 24 times in every draw.
All inputs are finite; a program needn't handle non-finite values.
Results may differ from a plain program's by a relative error of at most 0.0067.
Values may be sent and summed in bfloat16 or wider, within the bound.
No kernel may reach another device: no remote copies, remote signals or barrier semaphores. Data moves between devices by JAX's collectives and lax.ppermute only.
A program may use at most 128 MiB of HBM per device.

v0:
```python
import functools

import jax
import jax.numpy as jnp
from jax import lax
from jax.experimental import pallas as pl
from jax.experimental.pallas import tpu as pltpu
from jax.sharding import PartitionSpec as P


BLK = 256
SIDE = 4
CORES = 2
PAD = 128
AXES = ("dp", "cent")
SHIFTS = (0, 1, 3, 2)
FLOOR = -1e30


def device_at(plane, core, x, y):
    return (plane * CORES + core) * SIDE * SIDE + x * SIDE + y


def line_device(plane, core, row_pos, cent_pos):
    if core == 0:
        return device_at(plane, core, row_pos, cent_pos)
    return device_at(plane, core, cent_pos, row_pos)


def row_pairs(planes, shift):
    return [
        (line_device(z, c, (r + shift) % SIDE, k), line_device(z, c, r, k))
        for z in range(planes)
        for c in range(CORES)
        for r in range(SIDE)
        for k in range(SIDE)
    ]


def cent_pairs(planes, shift):
    return [
        (line_device(z, c, r, (k + shift) % SIDE), line_device(z, c, r, k))
        for z in range(planes)
        for c in range(CORES)
        for r in range(SIDE)
        for k in range(SIDE)
    ]


def row_lines(planes):
    return [
        [line_device(z, c, r, k) for r in range(SIDE)]
        for z in range(planes)
        for c in range(CORES)
        for k in range(SIDE)
    ]


def line_covers(planes):
    return [
        [line_device(z, c, r, k) for c in range(CORES) for z in range(planes) for k in range(SIDE)]
        for r in range(SIDE)
    ]


def split3(value):
    high = value.astype(jnp.bfloat16)
    rest = value - high.astype(jnp.float32)
    middle = rest.astype(jnp.bfloat16)
    low = (rest - middle.astype(jnp.float32)).astype(jnp.bfloat16)
    return high, middle, low


def tail_lanes(value):
    high, middle, low = (part.astype(jnp.float32) for part in split3(value))
    lane = lax.broadcasted_iota(jnp.int32, (value.shape[0], PAD), 1)
    tail = jnp.where(lane == 0, high, jnp.where(lane == 1, middle, jnp.where(lane == 2, low, 0.0)))
    return tail.astype(jnp.bfloat16)


def read_tail(ref, width):
    tail = ref[:, width:].astype(jnp.float32)
    return tail[:, 0:1] + tail[:, 1:2] + tail[:, 2:3]


def pack_kernel(cent_ref, out_ref):
    width = cent_ref.shape[1]
    values = cent_ref[...]
    out_ref[:, :width] = values.astype(jnp.bfloat16)
    out_ref[:, width:] = tail_lanes(0.5 * jnp.sum(values * values, axis=1, keepdims=True))


def score_kernel(scale, n_rows, extra, *refs):
    rows, cents = refs[:n_rows], refs[n_rows : n_rows + SIDE]
    before = refs[n_rows + SIDE : n_rows + SIDE + extra]
    exps = refs[n_rows + SIDE + extra : n_rows + 2 * SIDE + extra]
    stat_ref = refs[n_rows + 2 * SIDE + extra]
    width = rows[0].shape[1]
    base = 0
    for ref in before:
        stat_ref[base : base + ref.shape[0], :] = ref[...]
        base += ref.shape[0]
    for j in range(SIDE):
        half = read_tail(cents[j], width)
        start = 0
        for row_ref in rows:
            stop = start + row_ref.shape[0]
            dots = lax.dot_general(
                cents[j][:, :width],
                row_ref[...],
                (((1,), (1,)), ((), ())),
                preferred_element_type=jnp.float32,
            )
            logits = (dots - half) * scale
            peak = jnp.max(logits, axis=0, keepdims=True)
            exp_values = jnp.exp(logits - peak)
            exps[j][:, start:stop] = exp_values
            stat_ref[base + j : base + j + 1, start:stop] = peak
            stat_ref[base + SIDE + j : base + SIDE + j + 1, start:stop] = jnp.sum(
                exp_values, axis=0, keepdims=True
            )
            start = stop


def norm_kernel(pos_ref, all_ref, own_ref, scale_ref, log_ref, sum_ref):
    me = pos_ref[0]
    allow_base = 2 * SIDE

    def allowed(r):
        return all_ref[r, 0 : SIDE * SIDE, :]

    def stat_rows(ref, index):
        start = SIDE * SIDE + index * allow_base
        return ref[start : start + SIDE, :], ref[start + SIDE : start + 2 * SIDE, :]

    logs = []
    for r in range(SIDE):
        allow = allowed(r)
        peaks, totals = [], []
        for q in range(SIDE):
            peak, total = stat_rows(all_ref.at[q], SHIFTS.index((r - q) % SIDE))
            peaks.append(peak)
            totals.append(total)
        peak = jnp.concatenate(peaks, axis=0)
        total = jnp.concatenate(totals, axis=0)
        top = jnp.max(jnp.where(allow > 0, peak, FLOOR), axis=0, keepdims=True)
        parts = jnp.where(allow > 0, total * jnp.exp(jnp.minimum(peak - top, 0.0)), 0.0)
        logs.append(top + jnp.log(jnp.sum(parts, axis=0, keepdims=True)))
    row_sum = logs[0] + logs[1] + logs[2] + logs[3]
    sum_ref[...] = jnp.broadcast_to(jnp.sum(row_sum, axis=1, keepdims=True), sum_ref.shape)
    for t in range(SIDE):
        place = lax.rem(me + SHIFTS[t], SIDE)
        log_t = jnp.zeros_like(logs[0])
        allow_t = jnp.zeros((SIDE, log_t.shape[1]), jnp.float32)
        for r in range(SIDE):
            here = place == r
            log_t = jnp.where(here, logs[r], log_t)
            for q in range(SIDE):
                allow_t = jnp.where(
                    jnp.logical_and(here, me == q), allowed(r)[q * SIDE : (q + 1) * SIDE, :], allow_t
                )
        peak, _ = stat_rows(own_ref, t)
        scale_ref[t * SIDE : (t + 1) * SIDE, :] = jnp.where(
            allow_t > 0, jnp.exp(jnp.minimum(peak - log_t, 0.0)), 0.0
        )
        if t == 0:
            log_ref[...] = log_t


def weighted(j, scale_ref, exps, rows):
    total, lanes = None, None
    for t in range(SIDE):
        weights = exps[t][...] * scale_ref[t * SIDE + j : t * SIDE + j + 1, :]
        for start in range(0, weights.shape[1], PAD):
            piece = weights[:, start : start + PAD]
            lanes = piece if lanes is None else lanes + piece
        rounded = weights.astype(jnp.bfloat16)
        start = 0
        for row_ref in rows[t]:
            stop = start + row_ref.shape[0]
            term = jnp.dot(
                rounded[:, start:stop], row_ref[...], preferred_element_type=jnp.float32
            )
            total = term if total is None else total + term
            start = stop
    return total, jnp.sum(lanes, axis=1, keepdims=True)


def sums_kernel(scale_ref, *refs):
    n_rows = SIDE + 1
    flat, row_refs = refs[: SIDE * SIDE], refs[SIDE * SIDE : SIDE * SIDE + n_rows]
    outs = refs[SIDE * SIDE + n_rows :]
    rows = [[row_refs[0]], [row_refs[1]], [row_refs[2]], [row_refs[3], row_refs[4]]]
    width = row_refs[0].shape[1]
    for j in range(SIDE - 1, -1, -1):
        exps = [flat[t * SIDE + j] for t in range(SIDE)]
        total, counts = weighted(j, scale_ref, exps, rows)
        if j == 0:
            outs[0][...] = total
            outs[SIDE][...] = jnp.broadcast_to(counts, outs[SIDE].shape)
        else:
            outs[j][:, :width] = total.astype(jnp.bfloat16)
            outs[j][:, width:] = tail_lanes(counts)


def final_kernel(total_ref, count_ref, a_ref, b_ref, c_ref, old_ref, out_ref):
    width = total_ref.shape[1]
    total = total_ref[...] + old_ref[...]
    counts = count_ref[:, 0:1] + 1.0
    for ref in (a_ref, b_ref, c_ref):
        total = total + ref[:, :width].astype(jnp.float32)
        counts = counts + read_tail(ref, width)
    out_ref[...] = total / counts


def call(kernel, outs, n_in, limit, flops=0, nbytes=0, smem_first=False):
    vmem = pl.BlockSpec(memory_space=pltpu.VMEM)
    smem = pl.BlockSpec(memory_space=pltpu.SMEM)
    in_specs = [smem if smem_first and i == 0 else vmem for i in range(n_in)]
    return pl.pallas_call(
        kernel,
        out_shape=outs,
        in_specs=in_specs,
        out_specs=jax.tree.map(lambda _: vmem, outs),
        cost_estimate=pl.CostEstimate(flops=flops, bytes_accessed=nbytes, transcendentals=0),
        compiler_params=pltpu.CompilerParams(vmem_limit_bytes=limit << 20),
    )


def bulk(value, pairs):
    return lax.ppermute(value, AXES, pairs)


def step(embeddings, centroids, candidates):
    planes = lax.axis_size("dp") // CORES
    core = lax.axis_index("dp") % CORES
    cent_index = lax.axis_index("cent")
    x, y = cent_index // SIDE, cent_index % SIDE
    row_pos = jnp.where(core == 0, x, y)
    cent_pos = jnp.where(core == 0, y, x)
    row_len, width = embeddings.shape
    f32, bf16 = jnp.float32, jnp.bfloat16
    shape = jax.ShapeDtypeStruct

    packed = call(pack_kernel, shape((BLK, width + PAD), bf16), 1, 8, nbytes=2 << 20)(centroids)
    cents = [packed] + [bulk(packed, cent_pairs(planes, SHIFTS[t])) for t in range(1, SIDE)]
    near = bulk(embeddings, row_pairs(planes, 1))
    back = bulk(embeddings, row_pairs(planes, SIDE - 1))
    half = row_len // 2
    far = [bulk(near[:half], row_pairs(planes, 1)), bulk(back[half:], row_pairs(planes, SIDE - 1))]
    rows = [[embeddings], [near], [back], far]

    line = jnp.arange(SIDE, dtype=jnp.int32)
    other = (cent_pos + jnp.array(SHIFTS, jnp.int32)) % SIDE
    ids = jnp.where(
        core == 0, line[:, None] * SIDE + other[None, :], other[None, :] * SIDE + line[:, None]
    ).reshape(-1)
    allow = jnp.any(candidates[None] == ids[:, None, None], axis=2).astype(f32)
    allow = jnp.broadcast_to(
        allow[:, :, None], (SIDE * SIDE, candidates.shape[0], row_len // candidates.shape[0])
    ).reshape(SIDE * SIDE, row_len)

    exps, stats = [], [allow]
    pair_flops = 2 * row_len * SIDE * BLK * width
    for t in range(SIDE):
        extra = stats if t == SIDE - 1 else []
        stat_rows = 2 * SIDE + sum(part.shape[0] for part in extra)
        *exp_values, stat = call(
            functools.partial(score_kernel, 1.0 / width**0.5, len(rows[t]), len(extra)),
            [shape((BLK, row_len), f32)] * SIDE + [shape((stat_rows, row_len), f32)],
            len(rows[t]) + SIDE + len(extra),
            12,
            flops=pair_flops,
            nbytes=6 << 20,
        )(*rows[t], *cents, *extra)
        exps.append(exp_values)
        stats.append(stat)
    own_stats = stats[-1]
    all_stats = lax.all_gather(own_stats, AXES, axis_index_groups=row_lines(planes))
    n_cover = planes * CORES * SIDE
    scale, log_rows, line_sum = call(
        norm_kernel,
        [shape((SIDE * SIDE, row_len), f32), shape((1, row_len), f32), shape((n_cover, PAD), f32)],
        3,
        4,
        nbytes=1 << 20,
        smem_first=True,
    )(row_pos.reshape(1).astype(jnp.int32), all_stats, own_stats)

    total, *sent, counts = call(
        sums_kernel,
        [shape((BLK, width), f32)]
        + [shape((BLK, width + PAD), bf16)] * (SIDE - 1)
        + [shape((BLK, PAD), f32)],
        2 + SIDE * SIDE + SIDE,
        24,
        flops=SIDE * pair_flops,
        nbytes=16 << 20,
    )(scale, *[value for values in exps for value in values], *[part for parts in rows for part in parts])
    line_sum, sent, total, counts = lax.optimization_barrier((line_sum, sent, total, counts))
    cover_sums = lax.all_to_all(
        line_sum, AXES, 0, 0, tiled=True, axis_index_groups=line_covers(planes)
    )
    received = [bulk(sent[j - 1], cent_pairs(planes, -SHIFTS[j] % SIDE)) for j in (3, 1, 2)]
    tile = BLK // 2
    spec = lambda cols: pl.BlockSpec((tile, cols), lambda i: (i, 0))
    new_centroids = pl.pallas_call(
        final_kernel,
        name="final",
        grid=(BLK // tile,),
        out_shape=shape((BLK, width), f32),
        in_specs=[spec(width), spec(PAD)] + [spec(width + PAD)] * 3 + [spec(width)],
        out_specs=spec(width),
        cost_estimate=pl.CostEstimate(flops=0, bytes_accessed=5 << 20, transcendentals=0),
        compiler_params=pltpu.CompilerParams(vmem_limit_bytes=8 << 20),
    )(total, counts, *received, centroids)
    n_rows = row_len * lax.axis_size("dp") * SIDE * SIDE
    new_centroids, cover_sums = lax.optimization_barrier((new_centroids, cover_sums))
    objective = jnp.sum(cover_sums[:, 0]) / n_rows
    return new_centroids, log_rows.reshape(row_len), objective


def solution(mesh):
    in_specs = (P(AXES, None), P(AXES, None), P(AXES, None))
    out_specs = (P(AXES, None), P(AXES), P())
    return jax.shard_map(step, mesh=mesh, in_specs=in_specs, out_specs=out_specs, check_vma=False)
```

profile of v0, /device:TPU:1, one launch (start us, length us, event | category | flops | bytes accessed | tf_op | source)
XLA Modules:
  0.0 120.9 jit_solution(2591174097227561534)
XLA Ops:
  0.6 4.0 %collective-permute-start.2 = (bf16[512,1024]{1,0:T(8,128)(2,1)}, bf16[512,1024]{1,0:T(8,128)(2,1)S(1)}, u32[]{:S(2)}, u32[]{:S(2)}) collective-permute-start(bf16[512,1024]{1,0:T(8,128)(2,1)} %refs_16_.1), channel_id=1, source_target_pairs={{12,0},{13,1},{14,2},{15,3},{0,4},{1,5},{2,6},{3,7},{4,8},{5,9},{6... | collective-permute-start | bytes 3145736 | tf_op jit(solution)/shard_map/ppermute | solution.py:231
  4.7 3.4 %collective-permute-start = (bf16[512,1024]{1,0:T(8,128)(2,1)}, bf16[512,1024]{1,0:T(8,128)(2,1)S(1)}, u32[]{:S(2)}, u32[]{:S(2)}) collective-permute-start(bf16[512,1024]{1,0:T(8,128)(2,1)} %refs_16_.1), channel_id=1, source_target_pairs={{4,0},{5,1},{6,2},{7,3},{8,4},{9,5},{10,6},{11,7},{12,8},{13,9},{1... | collective-permute-start | bytes 3145736 | tf_op jit(solution)/shard_map/ppermute | solution.py:231
  8.0 1.2 %copy-done = f32[256,1024]{1,0:T(8,128)S(1)} copy-done((f32[256,1024]{1,0:T(8,128)S(1)}, f32[256,1024]{1,0:T(8,128)}, u32[]{:S(2)}) %copy-start) | copy-done | bytes 1048600
  9.4 4.7 %collective-permute-start.6 = (bf16[256,1152]{1,0:T(8,128)(2,1)S(1)}, bf16[256,1152]{1,0:T(8,128)(2,1)}, u32[]{:S(2)}, u32[]{:S(2)}) collective-permute-start(bf16[256,1152]{1,0:T(8,128)(2,1)S(1)} %shard_map.67.refs_1_.refs_2_), channel_id=1, source_target_pairs={{2,0},{3,1},{0,2},{1,3},{6,4},{7,5},{4,6},{5,7},{10,8},{11,9},{8,1... | collective-permute-start | bytes 1769480 | tf_op jit(solution)/shard_map/ppermute | solution.py:231
  14.1 2.2 %collective-permute-start.5 = (bf16[256,1152]{1,0:T(8,128)(2,1)S(1)}, bf16[256,1152]{1,0:T(8,128)(2,1)}, u32[]{:S(2)}, u32[]{:S(2)}) collective-permute-start(bf16[256,1152]{1,0:T(8,128)(2,1)S(1)} %shard_map.67.refs_1_.refs_2_), channel_id=1, source_target_pairs={{3,0},{0,1},{1,2},{2,3},{7,4},{4,5},{5,6},{6,7},{11,8},{8,9},{9,10... | collective-permute-start | bytes 1769480 | tf_op jit(solution)/shard_map/ppermute | solution.py:231
  16.3 4.3 %collective-permute-start.4 = (bf16[256,1152]{1,0:T(8,128)(2,1)S(1)}, bf16[256,1152]{1,0:T(8,128)(2,1)}, u32[]{:S(2)}, u32[]{:S(2)}) collective-permute-start(bf16[256,1152]{1,0:T(8,128)(2,1)S(1)} %shard_map.67.refs_1_.refs_2_), channel_id=1, source_target_pairs={{1,0},{2,1},{3,2},{0,3},{5,4},{6,5},{7,6},{4,7},{9,8},{10,9},{11,1... | collective-permute-start | bytes 1769480 | tf_op jit(solution)/shard_map/ppermute | solution.py:231
  22.1 1.9 %collective-permute-start.3 = (bf16[256,1024]{1,0:T(8,128)(2,1)}, bf16[256,1024]{1,0:T(8,128)(2,1)}, u32[]{:S(2)}, u32[]{:S(2)}) collective-permute-start(bf16[256,1024]{1,0:T(8,128)(2,1)} %slice.13), channel_id=1, source_target_pairs={{12,0},{13,1},{14,2},{15,3},{0,4},{1,5},{2,6},{3,7},{4,8},{5,9},{6... | collective-permute-start | bytes 1572872 | tf_op jit(solution)/shard_map/ppermute | solution.py:231
  24.1 0.9 slice.12
  25.0 7.8 %collective-permute-start.1 = (bf16[256,1024]{1,0:T(8,128)(2,1)}, bf16[256,1024]{1,0:T(8,128)(2,1)}, u32[]{:S(2)}, u32[]{:S(2)}) collective-permute-start(bf16[256,1024]{1,0:T(8,128)(2,1)} %slice.12), channel_id=1, source_target_pairs={{4,0},{5,1},{6,2},{7,3},{8,4},{9,5},{10,6},{11,7},{12,8},{13,9},{1... | collective-permute-start | bytes 1572872 | tf_op jit(solution)/shard_map/ppermute | solution.py:231
  33.8 3.0 %collective-permute-done.5.refs_3_.refs_4_ = bf16[256,1152]{1,0:T(8,128)(2,1)} collective-permute-done((bf16[256,1152]{1,0:T(8,128)(2,1)S(1)}, bf16[256,1152]{1,0:T(8,128)(2,1)}, u32[]{:S(2)}, u32[]{:S(2)}) %collective-permute-start.5) | collective-permute-done | bytes 589856 | tf_op jit(solution)/shard_map/ppermute | solution.py:231
  36.8 1.9 %collective-permute-done.4.refs_2_.refs_3_ = bf16[256,1152]{1,0:T(8,128)(2,1)} collective-permute-done((bf16[256,1152]{1,0:T(8,128)(2,1)S(1)}, bf16[256,1152]{1,0:T(8,128)(2,1)}, u32[]{:S(2)}, u32[]{:S(2)}) %collective-permute-start.4) | collective-permute-done | bytes 589856 | tf_op jit(solution)/shard_map/ppermute | solution.py:231
  38.7 1.2 %copy-done.4 = bf16[512,1024]{1,0:T(8,128)(2,1)S(1)} copy-done((bf16[512,1024]{1,0:T(8,128)(2,1)S(1)}, bf16[512,1024]{1,0:T(8,128)(2,1)}, u32[]{:S(2)}) %copy-start.4) | copy-done | bytes 1048600
  39.9 3.1 %shard_map.68 = (f32[256,512]{1,0:T(8,128)S(1)}, f32[256,512]{1,0:T(8,128)S(1)}, f32[256,512]{1,0:T(8,128)S(1)}, f32[256,512]{1,0:T(8,128)S(1)}, f32[8,512]{1,0:T(8,128)S(1)}) custom-call(bf16[512,1024]{1,0:T(8,128)(2,1)S(1)} %copy-done.4, bf16[256,1152]{1,0:T(8,128)(2,1)S(1)} %shard_map.67.refs_1_.refs_2_, ...), custom_call_target="tpu_custom_call" | custom-call | flops 1073741824 | bytes 6291456 | tf_op jit(solution)/shard_map/pallas_call | solution.py:268
  43.0 3.1 %shard_map.69 = (f32[256,512]{1,0:T(8,128)S(1)}, f32[256,512]{1,0:T(8,128)S(1)}, f32[256,512]{1,0:T(8,128)S(1)}, f32[256,512]{1,0:T(8,128)S(1)}, f32[8,512]{1,0:T(8,128)S(1)}) custom-call(bf16[512,1024]{1,0:T(8,128)(2,1)S(1)} %collective-permute-done.refs_0_.refs_17_, bf16[256,1152]{1,0:T(8,128)(2,1)S(1)} %shard_map.67.refs_1_.refs_2_, ...), custom_call_target="tpu_custom_call" | custom-call | flops 1073741824 | bytes 6291456 | tf_op jit(solution)/shard_map/pallas_call | solution.py:268
  46.1 3.1 %shard_map.70 = (f32[256,512]{1,0:T(8,128)S(1)}, f32[256,512]{1,0:T(8,128)S(1)}, f32[256,512]{1,0:T(8,128)S(1)}, f32[256,512]{1,0:T(8,128)S(1)}, f32[8,512]{1,0:T(8,128)S(1)}) custom-call(bf16[512,1024]{1,0:T(8,128)(2,1)S(1)} %collective-permute-done.2.refs_0_.refs_18_, bf16[256,1152]{1,0:T(8,128)(2,1)S(1)} %shard_map.67.refs_1_.refs_2_, ...), custom_call_target="tpu_custom_call" | custom-call | flops 1073741824 | bytes 6291456 | tf_op jit(solution)/shard_map/pallas_call | solution.py:268
  49.3 3.6 %shard_map.71 = (f32[256,512]{1,0:T(8,128)S(1)}, f32[256,512]{1,0:T(8,128)S(1)}, f32[256,512]{1,0:T(8,128)S(1)}, f32[256,512]{1,0:T(8,128)S(1)}, f32[48,512]{1,0:T(8,128)S(1)}) custom-call(bf16[256,1024]{1,0:T(8,128)(2,1)} %collective-permute-done.1.refs_0_.refs_19_, bf16[256,1024]{1,0:T(8,128)(2,1)} %collective-permute-done.3.refs_1_.refs_20_, ...), custom_call_target="tpu_custom_call" | custom-call | flops 1073741824 | bytes 6291456 | tf_op jit(solution)/shard_map/pallas_call | solution.py:268
  52.8 9.6 %all-gather = f32[192,512]{1,0:T(8,128)S(1)} all-gather(f32[48,512]{1,0:T(8,128)S(1)} %get-tuple-element.42.own_ref), channel_id=2, replica_groups={{0,4,8,12},{1,5,9,13},{2,6,10,14},{3,7,11,15},{16,17,18,19},{20,21,22,2..., dimensions={0}, use_global_device_ids=true | all-gather | bytes 491520 | tf_op jit(solution)/shard_map/all_gather | solution.py:279
  63.3 7.0 %shard_map.73 = (f32[256,1024]{1,0:T(8,128)S(1)}, bf16[256,1152]{1,0:T(8,128)(2,1)}, bf16[256,1152]{1,0:T(8,128)(2,1)}, bf16[256,1152]{1,0:T(8,128)(2,1)}, f32[256,128]{1,0:T(8,128)S(1)}) custom-call(f32[16,512]{1,0:T(8,128)S(1)} %get-tuple-element.44.scale_ref, f32[256,512]{1,0:T(8,128)S(1)} %get-tuple-element.45.refs_0_, ...), custom_call_target="tpu_custom_call" | custom-call | flops 4294967296 | bytes 16777216 | tf_op jit(solution)/shard_map/pallas_call | solution.py:290
  70.2 4.3 %collective-permute-start.7 = (bf16[256,1152]{1,0:T(8,128)(2,1)}, bf16[256,1152]{1,0:T(8,128)(2,1)S(1)}, u32[]{:S(2)}, u32[]{:S(2)}) collective-permute-start(bf16[256,1152]{1,0:T(8,128)(2,1)} %get-tuple-element.68), channel_id=1, source_target_pairs={{2,0},{3,1},{0,2},{1,3},{6,4},{7,5},{4,6},{5,7},{10,8},{11,9},{8,1... | collective-permute-start | bytes 1769480 | tf_op jit(solution)/shard_map/ppermute | solution.py:231
  74.5 1.9 %collective-permute-start.8 = (bf16[256,1152]{1,0:T(8,128)(2,1)}, bf16[256,1152]{1,0:T(8,128)(2,1)S(1)}, u32[]{:S(2)}, u32[]{:S(2)}) collective-permute-start(bf16[256,1152]{1,0:T(8,128)(2,1)} %get-tuple-element.69), channel_id=1, source_target_pairs={{3,0},{0,1},{1,2},{2,3},{7,4},{4,5},{5,6},{6,7},{11,8},{8,9},{9,10... | collective-permute-start | bytes 1769480 | tf_op jit(solution)/shard_map/ppermute | solution.py:231
  76.4 4.6 %collective-permute-start.9 = (bf16[256,1152]{1,0:T(8,128)(2,1)}, bf16[256,1152]{1,0:T(8,128)(2,1)}, u32[]{:S(2)}, u32[]{:S(2)}) collective-permute-start(bf16[256,1152]{1,0:T(8,128)(2,1)} %get-tuple-element.70), channel_id=1, source_target_pairs={{1,0},{2,1},{3,2},{0,3},{5,4},{6,5},{7,6},{4,7},{9,8},{10,9},{11,1... | collective-permute-start | bytes 1769480 | tf_op jit(solution)/shard_map/ppermute | solution.py:231
  81.0 22.7 %all-to-all-start = ((f32[128,1,128]{2,1,0:T(1,128)}), f32[128,1,128]{2,1,0:T(1,128)S(1)}, u32[]{:S(2)}, u32[]{:S(2)}) async-start(f32[128,1,128]{2,1,0:T(1,128)} %bitcast.3), calls=%async_computation | async-start | bytes 131072 | tf_op jit(solution)/shard_map/all_to_all | solution.py:301
  103.7 2.3 %final.1 = f32[256,1024]{1,0:T(8,128)} custom-call(f32[256,1024]{1,0:T(8,128)S(1)} %get-tuple-element.66.total_ref, f32[256,128]{1,0:T(8,128)S(1)} %get-tuple-element.67.count_ref, bf16[256,1152]{1,0:T(8,128)(2,1)S(1)} %collective-permute-done.7.a_ref, bf16[256,1152]{1,0:T(8,128)(2,1)S(1)} %collective-permute-done.8.b_ref, ...), custom_call_target="tpu_custom_call" | custom-call | bytes 5242880 | tf_op jit(solution)/shard_map/final/pallas_call | solution.py:307
  106.1 12.5 %all-to-all-done = f32[128,1,128]{2,1,0:T(1,128)S(1)} async-done(((f32[128,1,128]{2,1,0:T(1,128)}), f32[128,1,128]{2,1,0:T(1,128)S(1)}, u32[]{:S(2)}, u32[]{:S(2)}) %all-to-all-start) | async-done | bytes 65568 | tf_op jit(solution)/shard_map/all_to_all | solution.py:301
  (34 shorter events, 4.2 us)
Async XLA Ops:
  0.6 20.7 %collective-permute-start.2 = (bf16[512,1024]{1,0:T(8,128)(2,1)}, bf16[512,1024]{1,0:T(8,128)(2,1)S(1)}, u32[]{:S(2)}, u32[]{:S(2)}) collective-permute-start(bf16[512,1024]{1,0:T(8,128)(2,1)} %refs_16_.1), channel_id=1, source_target_pairs={{12,0},{13,1},{14,2},{15,3},{0,4},{1,5},{2,6},{3,7},{4,8},{5,9},{6... | collective-permute-start | bytes 3145736 | tf_op jit(solution)/shard_map/ppermute | solution.py:231
  4.7 19.4 %collective-permute-start = (bf16[512,1024]{1,0:T(8,128)(2,1)}, bf16[512,1024]{1,0:T(8,128)(2,1)S(1)}, u32[]{:S(2)}, u32[]{:S(2)}) collective-permute-start(bf16[512,1024]{1,0:T(8,128)(2,1)} %refs_16_.1), channel_id=1, source_target_pairs={{4,0},{5,1},{6,2},{7,3},{8,4},{9,5},{10,6},{11,7},{12,8},{13,9},{1... | collective-permute-start | bytes 3145736 | tf_op jit(solution)/shard_map/ppermute | solution.py:231
  8.0 1.2 %copy-start = (f32[256,1024]{1,0:T(8,128)S(1)}, f32[256,1024]{1,0:T(8,128)}, u32[]{:S(2)}) copy-start(f32[256,1024]{1,0:T(8,128)} %old_ref.1) | copy-start | bytes 3145732
  9.4 24.3 %collective-permute-start.6 = (bf16[256,1152]{1,0:T(8,128)(2,1)S(1)}, bf16[256,1152]{1,0:T(8,128)(2,1)}, u32[]{:S(2)}, u32[]{:S(2)}) collective-permute-start(bf16[256,1152]{1,0:T(8,128)(2,1)S(1)} %shard_map.67.refs_1_.refs_2_), channel_id=1, source_target_pairs={{2,0},{3,1},{0,2},{1,3},{6,4},{7,5},{4,6},{5,7},{10,8},{11,9},{8,1... | collective-permute-start | bytes 1769480 | tf_op jit(solution)/shard_map/ppermute | solution.py:231
  14.1 22.7 %collective-permute-start.5 = (bf16[256,1152]{1,0:T(8,128)(2,1)S(1)}, bf16[256,1152]{1,0:T(8,128)(2,1)}, u32[]{:S(2)}, u32[]{:S(2)}) collective-permute-start(bf16[256,1152]{1,0:T(8,128)(2,1)S(1)} %shard_map.67.refs_1_.refs_2_), channel_id=1, source_target_pairs={{3,0},{0,1},{1,2},{2,3},{7,4},{4,5},{5,6},{6,7},{11,8},{8,9},{9,10... | collective-permute-start | bytes 1769480 | tf_op jit(solution)/shard_map/ppermute | solution.py:231
  16.3 22.3 %collective-permute-start.4 = (bf16[256,1152]{1,0:T(8,128)(2,1)S(1)}, bf16[256,1152]{1,0:T(8,128)(2,1)}, u32[]{:S(2)}, u32[]{:S(2)}) collective-permute-start(bf16[256,1152]{1,0:T(8,128)(2,1)S(1)} %shard_map.67.refs_1_.refs_2_), channel_id=1, source_target_pairs={{1,0},{2,1},{3,2},{0,3},{5,4},{6,5},{7,6},{4,7},{9,8},{10,9},{11,1... | collective-permute-start | bytes 1769480 | tf_op jit(solution)/shard_map/ppermute | solution.py:231
  20.6 0.7 copy-start.7
  22.1 27.1 %collective-permute-start.3 = (bf16[256,1024]{1,0:T(8,128)(2,1)}, bf16[256,1024]{1,0:T(8,128)(2,1)}, u32[]{:S(2)}, u32[]{:S(2)}) collective-permute-start(bf16[256,1024]{1,0:T(8,128)(2,1)} %slice.13), channel_id=1, source_target_pairs={{12,0},{13,1},{14,2},{15,3},{0,4},{1,5},{2,6},{3,7},{4,8},{5,9},{6... | collective-permute-start | bytes 1572872 | tf_op jit(solution)/shard_map/ppermute | solution.py:231
  24.1 18.9 %copy-start.2 = (bf16[512,1024]{1,0:T(8,128)(2,1)}, bf16[512,1024]{1,0:T(8,128)(2,1)S(1)}, u32[]{:S(2)}) copy-start(bf16[512,1024]{1,0:T(8,128)(2,1)S(1)} %collective-permute-done.refs_0_.refs_17_) | copy-start | bytes 3145732
  25.0 24.3 %collective-permute-start.1 = (bf16[256,1024]{1,0:T(8,128)(2,1)}, bf16[256,1024]{1,0:T(8,128)(2,1)}, u32[]{:S(2)}, u32[]{:S(2)}) collective-permute-start(bf16[256,1024]{1,0:T(8,128)(2,1)} %slice.12), channel_id=1, source_target_pairs={{4,0},{5,1},{6,2},{7,3},{8,4},{9,5},{10,6},{11,7},{12,8},{13,9},{1... | collective-permute-start | bytes 1572872 | tf_op jit(solution)/shard_map/ppermute | solution.py:231
  32.8 0.7 copy-start.6
  38.7 1.2 %copy-start.4 = (bf16[512,1024]{1,0:T(8,128)(2,1)S(1)}, bf16[512,1024]{1,0:T(8,128)(2,1)}, u32[]{:S(2)}) copy-start(bf16[512,1024]{1,0:T(8,128)(2,1)} %refs_16_.1) | copy-start | bytes 3145732
  49.2 14.0 %copy-start.3 = (bf16[512,1024]{1,0:T(8,128)(2,1)S(1)}, bf16[512,1024]{1,0:T(8,128)(2,1)}, u32[]{:S(2)}) copy-start(bf16[512,1024]{1,0:T(8,128)(2,1)} %copy-done.2) | copy-start | bytes 3145732
  49.2 14.0 %copy-start.5 = (bf16[512,1024]{1,0:T(8,128)(2,1)S(1)}, bf16[512,1024]{1,0:T(8,128)(2,1)}, u32[]{:S(2)}) copy-start(bf16[512,1024]{1,0:T(8,128)(2,1)} %refs_16_.1) | copy-start | bytes 3145732
  63.3 40.5 %copy-start.1 = (f32[256,1024]{1,0:T(8,128)S(1)}, f32[256,1024]{1,0:T(8,128)}, u32[]{:S(2)}) copy-start(f32[256,1024]{1,0:T(8,128)} %old_ref.1) | copy-start | bytes 3145732
  70.2 33.5 %collective-permute-start.7 = (bf16[256,1152]{1,0:T(8,128)(2,1)}, bf16[256,1152]{1,0:T(8,128)(2,1)S(1)}, u32[]{:S(2)}, u32[]{:S(2)}) collective-permute-start(bf16[256,1152]{1,0:T(8,128)(2,1)} %get-tuple-element.68), channel_id=1, source_target_pairs={{2,0},{3,1},{0,2},{1,3},{6,4},{7,5},{4,6},{5,7},{10,8},{11,9},{8,1... | collective-permute-start | bytes 1769480 | tf_op jit(solution)/shard_map/ppermute | solution.py:231
  74.5 29.2 %collective-permute-start.8 = (bf16[256,1152]{1,0:T(8,128)(2,1)}, bf16[256,1152]{1,0:T(8,128)(2,1)S(1)}, u32[]{:S(2)}, u32[]{:S(2)}) collective-permute-start(bf16[256,1152]{1,0:T(8,128)(2,1)} %get-tuple-element.69), channel_id=1, source_target_pairs={{3,0},{0,1},{1,2},{2,3},{7,4},{4,5},{5,6},{6,7},{11,8},{8,9},{9,10... | collective-permute-start | bytes 1769480 | tf_op jit(solution)/shard_map/ppermute | solution.py:231
  76.4 27.3 %collective-permute-start.9 = (bf16[256,1152]{1,0:T(8,128)(2,1)}, bf16[256,1152]{1,0:T(8,128)(2,1)}, u32[]{:S(2)}, u32[]{:S(2)}) collective-permute-start(bf16[256,1152]{1,0:T(8,128)(2,1)} %get-tuple-element.70), channel_id=1, source_target_pairs={{1,0},{2,1},{3,2},{0,3},{5,4},{6,5},{7,6},{4,7},{9,8},{10,9},{11,1... | collective-permute-start | bytes 1769480 | tf_op jit(solution)/shard_map/ppermute | solution.py:231
  81.0 37.5 %all-to-all-start = ((f32[128,1,128]{2,1,0:T(1,128)}), f32[128,1,128]{2,1,0:T(1,128)S(1)}, u32[]{:S(2)}, u32[]{:S(2)}) async-start(f32[128,1,128]{2,1,0:T(1,128)} %bitcast.3), calls=%async_computation | async-start | bytes 131072 | tf_op jit(solution)/shard_map/all_to_all | solution.py:301
where the time goes:
time: 122 us; the launch traced here: 121 us
  starting transfers between devices  61.7 us (51%)
  Pallas kernels  23.1 us (19%)
  waiting for transfers between devices  17.3 us (14%)
  blocking collectives  9.63 us (8%)
  local copies, waits for them, and re-layouts  5.66 us (5%)
  between operations  2.67 us (2%)
    ppermute x10, starting transfers between devices, bulk(): return lax.ppermute(value, AXES, pairs)  39 us
    all_to_all x1, starting transfers between devices, step(): lax.all_to_all(line_sum, AXES, 0, 0, tiled=True, axis_index_groups=line_c...  22.7 us
    pallas_call x4, Pallas kernels, step(): call(functools.partial(score_kernel, 1.0 / width ** 0.5, len(rows[t]), le...  12.9 us
    all_to_all x1, waiting for transfers between devices, step(): lax.all_to_all(line_sum, AXES, 0, 0, tiled=True, axis_index_groups=line_c...  12.5 us
    all_gather x1, blocking collectives, step(): lax.all_gather(own_stats, AXES, axis_index_groups=row_lines(planes))  9.63 us
    pallas_call x1, Pallas kernels, step(): call(sums_kernel, [shape((BLK, width), f32)] + [shape((BLK, width + PAD),...  6.96 us
    ppermute x10, waiting for transfers between devices, bulk(): return lax.ppermute(value, AXES, pairs)  4.88 us
    unnamed x17, local copies, waits for them, and re-layouts  3.72 us
  transfers between devices with their start and end apart: 11, of which 3 were waited for; matrix products, arithmetic and copies ran while one was open for 2% of the time, Pallas kernels for 10%

commit v1 on v0

--- a/solution.py
+++ b/solution.py
@@ -90,13 +90,34 @@
     out_ref[:, width:] = tail_lanes(0.5 * jnp.sum(values * values, axis=1, keepdims=True))
 
 
-def score_kernel(scale, n_rows, extra, *refs):
+def allow_rows(pos_ref, list_ref, stat_ref):
+    core, cent_pos = pos_ref[1], pos_ref[2]
+    row_len = stat_ref.shape[1]
+    second = lax.broadcasted_iota(jnp.int32, (1, row_len), 1) >= row_len // 2
+    for q in range(SIDE):
+        for j in range(SIDE):
+            other = lax.rem(cent_pos + SHIFTS[j], SIDE)
+            block = jnp.where(core == 0, q * SIDE + other, other * SIDE + q)
+            hits = []
+            for b in range(list_ref.shape[0]):
+                hit = list_ref[b, 0] == block
+                for i in range(1, list_ref.shape[1]):
+                    hit = jnp.logical_or(hit, list_ref[b, i] == block)
+                hits.append(jnp.where(hit, 1.0, 0.0))
+            stat_ref[q * SIDE + j : q * SIDE + j + 1, :] = jnp.where(second, hits[1], hits[0])
+
+
+def first_score_kernel(scale, pos_ref, list_ref, *refs):
+    allow_rows(pos_ref, list_ref, refs[-1])
+    score_kernel(scale, 1, 0, *refs, base=SIDE * SIDE)
+
+
+def score_kernel(scale, n_rows, extra, *refs, base=0):
     rows, cents = refs[:n_rows], refs[n_rows : n_rows + SIDE]
     before = refs[n_rows + SIDE : n_rows + SIDE + extra]
     exps = refs[n_rows + SIDE + extra : n_rows + 2 * SIDE + extra]
     stat_ref = refs[n_rows + 2 * SIDE + extra]
     width = rows[0].shape[1]
-    base = 0
     for ref in before:
         stat_ref[base : base + ref.shape[0], :] = ref[...]
         base += ref.shape[0]
@@ -213,10 +234,10 @@
     out_ref[...] = total / counts
 
 
-def call(kernel, outs, n_in, limit, flops=0, nbytes=0, smem_first=False):
+def call(kernel, outs, n_in, limit, flops=0, nbytes=0, smem=0):
     vmem = pl.BlockSpec(memory_space=pltpu.VMEM)
-    smem = pl.BlockSpec(memory_space=pltpu.SMEM)
-    in_specs = [smem if smem_first and i == 0 else vmem for i in range(n_in)]
+    scalar = pl.BlockSpec(memory_space=pltpu.SMEM)
+    in_specs = [scalar] * smem + [vmem] * (n_in - smem)
     return pl.pallas_call(
         kernel,
         out_shape=outs,
@@ -250,29 +271,29 @@
     far = [bulk(near[:half], row_pairs(planes, 1)), bulk(back[half:], row_pairs(planes, SIDE - 1))]
     rows = [[embeddings], [near], [back], far]
 
-    line = jnp.arange(SIDE, dtype=jnp.int32)
-    other = (cent_pos + jnp.array(SHIFTS, jnp.int32)) % SIDE
-    ids = jnp.where(
-        core == 0, line[:, None] * SIDE + other[None, :], other[None, :] * SIDE + line[:, None]
-    ).reshape(-1)
-    allow = jnp.any(candidates[None] == ids[:, None, None], axis=2).astype(f32)
-    allow = jnp.broadcast_to(
-        allow[:, :, None], (SIDE * SIDE, candidates.shape[0], row_len // candidates.shape[0])
-    ).reshape(SIDE * SIDE, row_len)
-
-    exps, stats = [], [allow]
+    pos = jnp.stack([row_pos, core, cent_pos]).astype(jnp.int32)
+    exps, stats = [], []
     pair_flops = 2 * row_len * SIDE * BLK * width
     for t in range(SIDE):
         extra = stats if t == SIDE - 1 else []
         stat_rows = 2 * SIDE + sum(part.shape[0] for part in extra)
+        scalars = (pos, candidates) if t == 0 else ()
+        if t == 0:
+            stat_rows += SIDE * SIDE
+            kernel = functools.partial(first_score_kernel, 1.0 / width**0.5)
+        else:
+            kernel = functools.partial(
+                score_kernel, 1.0 / width**0.5, len(rows[t]), len(extra)
+            )
         *exp_values, stat = call(
-            functools.partial(score_kernel, 1.0 / width**0.5, len(rows[t]), len(extra)),
+            kernel,
             [shape((BLK, row_len), f32)] * SIDE + [shape((stat_rows, row_len), f32)],
-            len(rows[t]) + SIDE + len(extra),
+            len(scalars) + len(rows[t]) + SIDE + len(extra),
             12,
             flops=pair_flops,
             nbytes=6 << 20,
-        )(*rows[t], *cents, *extra)
+            smem=len(scalars),
+        )(*scalars, *rows[t], *cents, *extra)
         exps.append(exp_values)
         stats.append(stat)
     own_stats = stats[-1]
@@ -284,8 +305,8 @@
         3,
         4,
         nbytes=1 << 20,
-        smem_first=True,
-    )(row_pos.reshape(1).astype(jnp.int32), all_stats, own_stats)
+        smem=1,
+    )(pos, all_stats, own_stats)
 
     total, *sent, counts = call(
         sums_kernel,
@@ -297,7 +318,7 @@
         flops=SIDE * pair_flops,
         nbytes=16 << 20,
     )(scale, *[value for values in exps for value in values], *[part for parts in rows for part in parts])
-    line_sum, sent, total, counts = lax.optimization_barrier((line_sum, sent, total, counts))
+    line_sum, total = lax.optimization_barrier((line_sum, total))
     cover_sums = lax.all_to_all(
         line_sum, AXES, 0, 0, tiled=True, axis_index_groups=line_covers(planes)
     )

time: 122 us -> 122 us (level)
  waiting for transfers between devices: 17.3 us -> 18.9 us
  local copies, waits for them, and re-layouts: 5.66 us -> 4.17 us
    ppermute x10, waiting for transfers between devices: 4.88 us -> 6.45 us  [bulk(): return lax.ppermute(value, AXES, pairs)]
    unnamed x17 -> x14, local copies, waits for them, and re-layouts: 3.72 us -> 2.47 us
  transfers between devices with their start and end apart: 11 -> 11, of which waited for: 3 -> 4; matrix products, arithmetic and copies ran while one was open for 2% -> 1% of each run, Pallas kernels for 10% -> 10%
where the time goes in v1:
time: 122 us; the launch traced here: 121 us
  starting transfers between devices  61.4 us (50%)
  Pallas kernels  23.7 us (19%)
  waiting for transfers between devices  18.9 us (15%)
  blocking collectives  9.63 us (8%)
  local copies, waits for them, and re-layouts  4.17 us (3%)
  between operations  2.64 us (2%)
    ppermute x10, starting transfers between devices, bulk(): return lax.ppermute(value, AXES, pairs)  39.1 us
    all_to_all x1, starting transfers between devices, step(): lax.all_to_all(line_sum, AXES, 0, 0, tiled=True, axis_index_groups=line_c...  22.3 us
    pallas_call x4, Pallas kernels, step(): call(kernel, [shape((BLK, row_len), f32)] * SIDE + [shape((stat_rows, row...  12.9 us
    all_to_all x1, waiting for transfers between devices, step(): lax.all_to_all(line_sum, AXES, 0, 0, tiled=True, axis_index_groups=line_c...  12.5 us
    all_gather x1, blocking collectives, step(): lax.all_gather(own_stats, AXES, axis_index_groups=row_lines(planes))  9.63 us
    pallas_call x1, Pallas kernels, step(): call(sums_kernel, [shape((BLK, width), f32)] + [shape((BLK, width + PAD),...  6.96 us
    ppermute x10, waiting for transfers between devices, bulk(): return lax.ppermute(value, AXES, pairs)  6.45 us
    unnamed x14, local copies, waits for them, and re-layouts  2.47 us
  transfers between devices with their start and end apart: 11, of which 4 were waited for; matrix products, arithmetic and copies ran while one was open for 1% of the time, Pallas kernels for 10%

profile of v1, /device:TPU:1, one launch (start us, length us, event | category | flops | bytes accessed | tf_op | source)
XLA Modules:
  0.0 121.2 jit_solution(10074394347842253928)
XLA Ops:
  0.6 4.0 %collective-permute-start.2 = (bf16[512,1024]{1,0:T(8,128)(2,1)}, bf16[512,1024]{1,0:T(8,128)(2,1)S(1)}, u32[]{:S(2)}, u32[]{:S(2)}) collective-permute-start(bf16[512,1024]{1,0:T(8,128)(2,1)} %refs_16_.1), channel_id=1, source_target_pairs={{12,0},{13,1},{14,2},{15,3},{0,4},{1,5},{2,6},{3,7},{4,8},{5,9},{6... | collective-permute-start | bytes 3145736 | tf_op jit(solution)/shard_map/ppermute | solution.py:252
  4.7 3.4 %collective-permute-start = (bf16[512,1024]{1,0:T(8,128)(2,1)}, bf16[512,1024]{1,0:T(8,128)(2,1)S(1)}, u32[]{:S(2)}, u32[]{:S(2)}) collective-permute-start(bf16[512,1024]{1,0:T(8,128)(2,1)} %refs_16_.1), channel_id=1, source_target_pairs={{4,0},{5,1},{6,2},{7,3},{8,4},{9,5},{10,6},{11,7},{12,8},{13,9},{1... | collective-permute-start | bytes 3145736 | tf_op jit(solution)/shard_map/ppermute | solution.py:252
  8.0 1.2 %copy-done = f32[256,1024]{1,0:T(8,128)S(1)} copy-done((f32[256,1024]{1,0:T(8,128)S(1)}, f32[256,1024]{1,0:T(8,128)}, u32[]{:S(2)}) %copy-start) | copy-done | bytes 1048600
  9.4 4.7 %collective-permute-start.6 = (bf16[256,1152]{1,0:T(8,128)(2,1)S(1)}, bf16[256,1152]{1,0:T(8,128)(2,1)}, u32[]{:S(2)}, u32[]{:S(2)}) collective-permute-start(bf16[256,1152]{1,0:T(8,128)(2,1)S(1)} %shard_map.58.refs_1_.refs_2_), channel_id=1, source_target_pairs={{2,0},{3,1},{0,2},{1,3},{6,4},{7,5},{4,6},{5,7},{10,8},{11,9},{8,1... | collective-permute-start | bytes 1769480 | tf_op jit(solution)/shard_map/ppermute | solution.py:252
  14.1 2.2 %collective-permute-start.5 = (bf16[256,1152]{1,0:T(8,128)(2,1)S(1)}, bf16[256,1152]{1,0:T(8,128)(2,1)}, u32[]{:S(2)}, u32[]{:S(2)}) collective-permute-start(bf16[256,1152]{1,0:T(8,128)(2,1)S(1)} %shard_map.58.refs_1_.refs_2_), channel_id=1, source_target_pairs={{3,0},{0,1},{1,2},{2,3},{7,4},{4,5},{5,6},{6,7},{11,8},{8,9},{9,10... | collective-permute-start | bytes 1769480 | tf_op jit(solution)/shard_map/ppermute | solution.py:252
  16.3 4.3 %collective-permute-start.4 = (bf16[256,1152]{1,0:T(8,128)(2,1)S(1)}, bf16[256,1152]{1,0:T(8,128)(2,1)}, u32[]{:S(2)}, u32[]{:S(2)}) collective-permute-start(bf16[256,1152]{1,0:T(8,128)(2,1)S(1)} %shard_map.58.refs_1_.refs_2_), channel_id=1, source_target_pairs={{1,0},{2,1},{3,2},{0,3},{5,4},{6,5},{7,6},{4,7},{9,8},{10,9},{11,1... | collective-permute-start | bytes 1769480 | tf_op jit(solution)/shard_map/ppermute | solution.py:252
  21.4 1.9 %collective-permute-start.3 = (bf16[256,1024]{1,0:T(8,128)(2,1)}, bf16[256,1024]{1,0:T(8,128)(2,1)}, u32[]{:S(2)}, u32[]{:S(2)}) collective-permute-start(bf16[256,1024]{1,0:T(8,128)(2,1)} %slice.13), channel_id=1, source_target_pairs={{12,0},{13,1},{14,2},{15,3},{0,4},{1,5},{2,6},{3,7},{4,8},{5,9},{6... | collective-permute-start | bytes 1572872 | tf_op jit(solution)/shard_map/ppermute | solution.py:252
  24.9 7.8 %collective-permute-start.1 = (bf16[256,1024]{1,0:T(8,128)(2,1)}, bf16[256,1024]{1,0:T(8,128)(2,1)}, u32[]{:S(2)}, u32[]{:S(2)}) collective-permute-start(bf16[256,1024]{1,0:T(8,128)(2,1)} %slice.12), channel_id=1, source_target_pairs={{4,0},{5,1},{6,2},{7,3},{8,4},{9,5},{10,6},{11,7},{12,8},{13,9},{1... | collective-permute-start | bytes 1572872 | tf_op jit(solution)/shard_map/ppermute | solution.py:252
  32.9 3.9 %collective-permute-done.5.refs_3_.refs_4_ = bf16[256,1152]{1,0:T(8,128)(2,1)} collective-permute-done((bf16[256,1152]{1,0:T(8,128)(2,1)S(1)}, bf16[256,1152]{1,0:T(8,128)(2,1)}, u32[]{:S(2)}, u32[]{:S(2)}) %collective-permute-start.5) | collective-permute-done | bytes 589856 | tf_op jit(solution)/shard_map/ppermute | solution.py:252
  36.8 1.9 %collective-permute-done.4.refs_2_.refs_3_ = bf16[256,1152]{1,0:T(8,128)(2,1)} collective-permute-done((bf16[256,1152]{1,0:T(8,128)(2,1)S(1)}, bf16[256,1152]{1,0:T(8,128)(2,1)}, u32[]{:S(2)}, u32[]{:S(2)}) %collective-permute-start.4) | collective-permute-done | bytes 589856 | tf_op jit(solution)/shard_map/ppermute | solution.py:252
  38.7 1.2 %copy-done.4 = bf16[512,1024]{1,0:T(8,128)(2,1)S(1)} copy-done((bf16[512,1024]{1,0:T(8,128)(2,1)S(1)}, bf16[512,1024]{1,0:T(8,128)(2,1)}, u32[]{:S(2)}) %copy-start.4) | copy-done | bytes 1048600
  39.9 3.2 %shard_map.59 = (f32[256,512]{1,0:T(8,128)S(1)}, f32[256,512]{1,0:T(8,128)S(1)}, f32[256,512]{1,0:T(8,128)S(1)}, f32[256,512]{1,0:T(8,128)S(1)}, f32[24,512]{1,0:T(8,128)S(1)}) custom-call(s32[3]{0:T(128)S(1)} %pad_add_fusion.pos_ref, s32[2,8]{1,0:T(2,128)S(1)} %copy-done.6, bf16[512,1024]{1,0:T(8,128)(2,1)S(1)} %copy-done.4, ...), custom_call_target="tpu_custom_call" | custom-call | flops 1073741824 | bytes 6291456 | tf_op jit(solution)/shard_map/pallas_call | solution.py:288
  43.1 3.1 %shard_map.60 = (f32[256,512]{1,0:T(8,128)S(1)}, f32[256,512]{1,0:T(8,128)S(1)}, f32[256,512]{1,0:T(8,128)S(1)}, f32[256,512]{1,0:T(8,128)S(1)}, f32[8,512]{1,0:T(8,128)S(1)}) custom-call(bf16[512,1024]{1,0:T(8,128)(2,1)S(1)} %collective-permute-done.refs_0_.refs_17_, bf16[256,1152]{1,0:T(8,128)(2,1)S(1)} %shard_map.58.refs_1_.refs_2_, ...), custom_call_target="tpu_custom_call" | custom-call | flops 1073741824 | bytes 6291456 | tf_op jit(solution)/shard_map/pallas_call | solution.py:288
  46.2 3.1 %shard_map.61 = (f32[256,512]{1,0:T(8,128)S(1)}, f32[256,512]{1,0:T(8,128)S(1)}, f32[256,512]{1,0:T(8,128)S(1)}, f32[256,512]{1,0:T(8,128)S(1)}, f32[8,512]{1,0:T(8,128)S(1)}) custom-call(bf16[512,1024]{1,0:T(8,128)(2,1)S(1)} %collective-permute-done.2.refs_0_.refs_18_, bf16[256,1152]{1,0:T(8,128)(2,1)S(1)} %shard_map.58.refs_1_.refs_2_, ...), custom_call_target="tpu_custom_call" | custom-call | flops 1073741824 | bytes 6291456 | tf_op jit(solution)/shard_map/pallas_call | solution.py:288
  49.3 3.6 %shard_map.62 = (f32[256,512]{1,0:T(8,128)S(1)}, f32[256,512]{1,0:T(8,128)S(1)}, f32[256,512]{1,0:T(8,128)S(1)}, f32[256,512]{1,0:T(8,128)S(1)}, f32[48,512]{1,0:T(8,128)S(1)}) custom-call(bf16[256,1024]{1,0:T(8,128)(2,1)} %collective-permute-done.1.refs_0_.refs_19_, bf16[256,1024]{1,0:T(8,128)(2,1)} %collective-permute-done.3.refs_1_.refs_20_, ...), custom_call_target="tpu_custom_call" | custom-call | flops 1073741824 | bytes 6291456 | tf_op jit(solution)/shard_map/pallas_call | solution.py:288
  52.9 9.6 %all-gather = f32[192,512]{1,0:T(8,128)S(1)} all-gather(f32[48,512]{1,0:T(8,128)S(1)} %get-tuple-element.38.own_ref), channel_id=2, replica_groups={{0,4,8,12},{1,5,9,13},{2,6,10,14},{3,7,11,15},{16,17,18,19},{20,21,22,2..., dimensions={0}, use_global_device_ids=true | all-gather | bytes 491520 | tf_op jit(solution)/shard_map/all_gather | solution.py:300
  62.5 1.3 %shard_map.63 = (f32[16,512]{1,0:T(8,128)S(1)}, f32[1,512]{1,0:T(1,128)}, f32[128,128]{1,0:T(8,128)}) custom-call(s32[3]{0:T(128)S(1)} %pad_add_fusion.pos_ref, f32[4,48,512]{2,1,0:T(8,128)S(1)} %bitcast.9, f32[48,512]{1,0:T(8,128)S(1)} %get-tuple-element.38.own_ref), custom_call_target="tpu_custom_call" | custom-call | bytes 1048576 | tf_op jit(solution)/shard_map/pallas_call | solution.py:302
  63.9 7.0 %shard_map.64 = (f32[256,1024]{1,0:T(8,128)S(1)}, bf16[256,1152]{1,0:T(8,128)(2,1)}, bf16[256,1152]{1,0:T(8,128)(2,1)}, bf16[256,1152]{1,0:T(8,128)(2,1)}, f32[256,128]{1,0:T(8,128)S(1)}) custom-call(f32[16,512]{1,0:T(8,128)S(1)} %get-tuple-element.40.scale_ref, f32[256,512]{1,0:T(8,128)S(1)} %get-tuple-element.41.refs_0_, ...), custom_call_target="tpu_custom_call" | custom-call | flops 4294967296 | bytes 16777216 | tf_op jit(solution)/shard_map/pallas_call | solution.py:311
  70.8 4.3 %collective-permute-start.7 = (bf16[256,1152]{1,0:T(8,128)(2,1)}, bf16[256,1152]{1,0:T(8,128)(2,1)S(1)}, u32[]{:S(2)}, u32[]{:S(2)}) collective-permute-start(bf16[256,1152]{1,0:T(8,128)(2,1)} %get-tuple-element.60), channel_id=1, source_target_pairs={{2,0},{3,1},{0,2},{1,3},{6,4},{7,5},{4,6},{5,7},{10,8},{11,9},{8,1... | collective-permute-start | bytes 1769480 | tf_op jit(solution)/shard_map/ppermute | solution.py:252
  75.1 1.9 %collective-permute-start.8 = (bf16[256,1152]{1,0:T(8,128)(2,1)}, bf16[256,1152]{1,0:T(8,128)(2,1)S(1)}, u32[]{:S(2)}, u32[]{:S(2)}) collective-permute-start(bf16[256,1152]{1,0:T(8,128)(2,1)} %get-tuple-element.61), channel_id=1, source_target_pairs={{3,0},{0,1},{1,2},{2,3},{7,4},{4,5},{5,6},{6,7},{11,8},{8,9},{9,10... | collective-permute-start | bytes 1769480 | tf_op jit(solution)/shard_map/ppermute | solution.py:252
  77.1 4.6 %collective-permute-start.9 = (bf16[256,1152]{1,0:T(8,128)(2,1)}, bf16[256,1152]{1,0:T(8,128)(2,1)}, u32[]{:S(2)}, u32[]{:S(2)}) collective-permute-start(bf16[256,1152]{1,0:T(8,128)(2,1)} %get-tuple-element.62), channel_id=1, source_target_pairs={{1,0},{2,1},{3,2},{0,3},{5,4},{6,5},{7,6},{4,7},{9,8},{10,9},{11,1... | collective-permute-start | bytes 1769480 | tf_op jit(solution)/shard_map/ppermute | solution.py:252
  81.6 22.3 %all-to-all-start = ((f32[128,1,128]{2,1,0:T(1,128)}), f32[128,1,128]{2,1,0:T(1,128)S(1)}, u32[]{:S(2)}, u32[]{:S(2)}) async-start(f32[128,1,128]{2,1,0:T(1,128)} %bitcast.5), calls=%async_computation | async-start | bytes 131072 | tf_op jit(solution)/shard_map/all_to_all | solution.py:322
  104.0 2.3 %final.1 = f32[256,1024]{1,0:T(8,128)} custom-call(f32[256,1024]{1,0:T(8,128)S(1)} %get-tuple-element.58.total_ref, f32[256,128]{1,0:T(8,128)S(1)} %get-tuple-element.59.count_ref, bf16[256,1152]{1,0:T(8,128)(2,1)S(1)} %collective-permute-done.7.a_ref, bf16[256,1152]{1,0:T(8,128)(2,1)S(1)} %collective-permute-done.8.b_ref, ...), custom_call_target="tpu_custom_call" | custom-call | bytes 5242880 | tf_op jit(solution)/shard_map/final/pallas_call | solution.py:328
  106.3 12.5 %all-to-all-done = f32[128,1,128]{2,1,0:T(1,128)S(1)} async-done(((f32[128,1,128]{2,1,0:T(1,128)}), f32[128,1,128]{2,1,0:T(1,128)S(1)}, u32[]{:S(2)}, u32[]{:S(2)}) %all-to-all-start) | async-done | bytes 65568 | tf_op jit(solution)/shard_map/all_to_all | solution.py:322
  (25 shorter events, 3.3 us)
Async XLA Ops:
  0.6 20.0 %collective-permute-start.2 = (bf16[512,1024]{1,0:T(8,128)(2,1)}, bf16[512,1024]{1,0:T(8,128)(2,1)S(1)}, u32[]{:S(2)}, u32[]{:S(2)}) collective-permute-start(bf16[512,1024]{1,0:T(8,128)(2,1)} %refs_16_.1), channel_id=1, source_target_pairs={{12,0},{13,1},{14,2},{15,3},{0,4},{1,5},{2,6},{3,7},{4,8},{5,9},{6... | collective-permute-start | bytes 3145736 | tf_op jit(solution)/shard_map/ppermute | solution.py:252
  4.7 19.4 %collective-permute-start = (bf16[512,1024]{1,0:T(8,128)(2,1)}, bf16[512,1024]{1,0:T(8,128)(2,1)S(1)}, u32[]{:S(2)}, u32[]{:S(2)}) collective-permute-start(bf16[512,1024]{1,0:T(8,128)(2,1)} %refs_16_.1), channel_id=1, source_target_pairs={{4,0},{5,1},{6,2},{7,3},{8,4},{9,5},{10,6},{11,7},{12,8},{13,9},{1... | collective-permute-start | bytes 3145736 | tf_op jit(solution)/shard_map/ppermute | solution.py:252
  8.0 1.2 %copy-start = (f32[256,1024]{1,0:T(8,128)S(1)}, f32[256,1024]{1,0:T(8,128)}, u32[]{:S(2)}) copy-start(f32[256,1024]{1,0:T(8,128)} %old_ref.1) | copy-start | bytes 3145732
  9.4 23.4 %collective-permute-start.6 = (bf16[256,1152]{1,0:T(8,128)(2,1)S(1)}, bf16[256,1152]{1,0:T(8,128)(2,1)}, u32[]{:S(2)}, u32[]{:S(2)}) collective-permute-start(bf16[256,1152]{1,0:T(8,128)(2,1)S(1)} %shard_map.58.refs_1_.refs_2_), channel_id=1, source_target_pairs={{2,0},{3,1},{0,2},{1,3},{6,4},{7,5},{4,6},{5,7},{10,8},{11,9},{8,1... | collective-permute-start | bytes 1769480 | tf_op jit(solution)/shard_map/ppermute | solution.py:252
  14.1 22.7 %collective-permute-start.5 = (bf16[256,1152]{1,0:T(8,128)(2,1)S(1)}, bf16[256,1152]{1,0:T(8,128)(2,1)}, u32[]{:S(2)}, u32[]{:S(2)}) collective-permute-start(bf16[256,1152]{1,0:T(8,128)(2,1)S(1)} %shard_map.58.refs_1_.refs_2_), channel_id=1, source_target_pairs={{3,0},{0,1},{1,2},{2,3},{7,4},{4,5},{5,6},{6,7},{11,8},{8,9},{9,10... | collective-permute-start | bytes 1769480 | tf_op jit(solution)/shard_map/ppermute | solution.py:252
  16.3 22.3 %collective-permute-start.4 = (bf16[256,1152]{1,0:T(8,128)(2,1)S(1)}, bf16[256,1152]{1,0:T(8,128)(2,1)}, u32[]{:S(2)}, u32[]{:S(2)}) collective-permute-start(bf16[256,1152]{1,0:T(8,128)(2,1)S(1)} %shard_map.58.refs_1_.refs_2_), channel_id=1, source_target_pairs={{1,0},{2,1},{3,2},{0,3},{5,4},{6,5},{7,6},{4,7},{9,8},{10,9},{11,1... | collective-permute-start | bytes 1769480 | tf_op jit(solution)/shard_map/ppermute | solution.py:252
  21.4 27.8 %collective-permute-start.3 = (bf16[256,1024]{1,0:T(8,128)(2,1)}, bf16[256,1024]{1,0:T(8,128)(2,1)}, u32[]{:S(2)}, u32[]{:S(2)}) collective-permute-start(bf16[256,1024]{1,0:T(8,128)(2,1)} %slice.13), channel_id=1, source_target_pairs={{12,0},{13,1},{14,2},{15,3},{0,4},{1,5},{2,6},{3,7},{4,8},{5,9},{6... | collective-permute-start | bytes 1572872 | tf_op jit(solution)/shard_map/ppermute | solution.py:252
  24.0 19.0 %copy-start.2 = (bf16[512,1024]{1,0:T(8,128)(2,1)}, bf16[512,1024]{1,0:T(8,128)(2,1)S(1)}, u32[]{:S(2)}) copy-start(bf16[512,1024]{1,0:T(8,128)(2,1)S(1)} %collective-permute-done.refs_0_.refs_17_) | copy-start | bytes 3145732
  24.9 24.4 %collective-permute-start.1 = (bf16[256,1024]{1,0:T(8,128)(2,1)}, bf16[256,1024]{1,0:T(8,128)(2,1)}, u32[]{:S(2)}, u32[]{:S(2)}) collective-permute-start(bf16[256,1024]{1,0:T(8,128)(2,1)} %slice.12), channel_id=1, source_target_pairs={{4,0},{5,1},{6,2},{7,3},{8,4},{9,5},{10,6},{11,7},{12,8},{13,9},{1... | collective-permute-start | bytes 1572872 | tf_op jit(solution)/shard_map/ppermute | solution.py:252
  32.8 5.9 %copy-start.6 = (s32[2,8]{1,0:T(2,128)S(1)}, s32[2,8]{1,0:T(2,128)}, u32[]{:S(2)}) copy-start(s32[2,8]{1,0:T(2,128)} %list_ref.1) | copy-start | bytes 196
  38.7 1.2 %copy-start.4 = (bf16[512,1024]{1,0:T(8,128)(2,1)S(1)}, bf16[512,1024]{1,0:T(8,128)(2,1)}, u32[]{:S(2)}) copy-start(bf16[512,1024]{1,0:T(8,128)(2,1)} %refs_16_.1) | copy-start | bytes 3145732
  49.3 14.6 %copy-start.3 = (bf16[512,1024]{1,0:T(8,128)(2,1)S(1)}, bf16[512,1024]{1,0:T(8,128)(2,1)}, u32[]{:S(2)}) copy-start(bf16[512,1024]{1,0:T(8,128)(2,1)} %copy-done.2) | copy-start | bytes 3145732
  49.3 14.6 %copy-start.5 = (bf16[512,1024]{1,0:T(8,128)(2,1)S(1)}, bf16[512,1024]{1,0:T(8,128)(2,1)}, u32[]{:S(2)}) copy-start(bf16[512,1024]{1,0:T(8,128)(2,1)} %refs_16_.1) | copy-start | bytes 3145732
  63.9 40.1 %copy-start.1 = (f32[256,1024]{1,0:T(8,128)S(1)}, f32[256,1024]{1,0:T(8,128)}, u32[]{:S(2)}) copy-start(f32[256,1024]{1,0:T(8,128)} %old_ref.1) | copy-start | bytes 3145732
  70.8 33.1 %collective-permute-start.7 = (bf16[256,1152]{1,0:T(8,128)(2,1)}, bf16[256,1152]{1,0:T(8,128)(2,1)S(1)}, u32[]{:S(2)}, u32[]{:S(2)}) collective-permute-start(bf16[256,1152]{1,0:T(8,128)(2,1)} %get-tuple-element.60), channel_id=1, source_target_pairs={{2,0},{3,1},{0,2},{1,3},{6,4},{7,5},{4,6},{5,7},{10,8},{11,9},{8,1... | collective-permute-start | bytes 1769480 | tf_op jit(solution)/shard_map/ppermute | solution.py:252
  75.1 28.8 %collective-permute-start.8 = (bf16[256,1152]{1,0:T(8,128)(2,1)}, bf16[256,1152]{1,0:T(8,128)(2,1)S(1)}, u32[]{:S(2)}, u32[]{:S(2)}) collective-permute-start(bf16[256,1152]{1,0:T(8,128)(2,1)} %get-tuple-element.61), channel_id=1, source_target_pairs={{3,0},{0,1},{1,2},{2,3},{7,4},{4,5},{5,6},{6,7},{11,8},{8,9},{9,10... | collective-permute-start | bytes 1769480 | tf_op jit(solution)/shard_map/ppermute | solution.py:252
  77.1 26.9 %collective-permute-start.9 = (bf16[256,1152]{1,0:T(8,128)(2,1)}, bf16[256,1152]{1,0:T(8,128)(2,1)}, u32[]{:S(2)}, u32[]{:S(2)}) collective-permute-start(bf16[256,1152]{1,0:T(8,128)(2,1)} %get-tuple-element.62), channel_id=1, source_target_pairs={{1,0},{2,1},{3,2},{0,3},{5,4},{6,5},{7,6},{4,7},{9,8},{10,9},{11,1... | collective-permute-start | bytes 1769480 | tf_op jit(solution)/shard_map/ppermute | solution.py:252
  81.6 37.1 %all-to-all-start = ((f32[128,1,128]{2,1,0:T(1,128)}), f32[128,1,128]{2,1,0:T(1,128)S(1)}, u32[]{:S(2)}, u32[]{:S(2)}) async-start(f32[128,1,128]{2,1,0:T(1,128)} %bitcast.5), calls=%async_computation | async-start | bytes 131072 | tf_op jit(solution)/shard_map/all_to_all | solution.py:322

commit v2 on v1

--- a/solution.py
+++ b/solution.py
@@ -15,6 +15,8 @@
 AXES = ("dp", "cent")
 SHIFTS = (0, 1, 3, 2)
 FLOOR = -1e30
+NEAR = ((0, None), (1, 1), (2, 0), (3, 0), (3, 1))
+FAR = ((1, 0), (2, 1))
 
 
 def device_at(plane, core, x, y):
@@ -29,7 +31,7 @@
 
 def row_pairs(planes, shift):
     return [
-        (line_device(z, c, (r + shift) % SIDE, k), line_device(z, c, r, k))
+        (line_device(z, c, r ^ shift, k), line_device(z, c, r, k))
         for z in range(planes)
         for c in range(CORES)
         for r in range(SIDE)
@@ -39,7 +41,7 @@
 
 def cent_pairs(planes, shift):
     return [
-        (line_device(z, c, r, (k + shift) % SIDE), line_device(z, c, r, k))
+        (line_device(z, c, r, k ^ shift), line_device(z, c, r, k))
         for z in range(planes)
         for c in range(CORES)
         for r in range(SIDE)
@@ -90,13 +92,25 @@
     out_ref[:, width:] = tail_lanes(0.5 * jnp.sum(values * values, axis=1, keepdims=True))
 
 
+def split_kernel(row_ref, first_ref, second_ref, sems):
+    half = first_ref.shape[0]
+    copies = [
+        pltpu.make_async_copy(row_ref.at[pl.ds(i * half, half), :], out_ref, sems.at[i])
+        for i, out_ref in enumerate((first_ref, second_ref))
+    ]
+    for copy in copies:
+        copy.start()
+    for copy in copies:
+        copy.wait()
+
+
 def allow_rows(pos_ref, list_ref, stat_ref):
     core, cent_pos = pos_ref[1], pos_ref[2]
     row_len = stat_ref.shape[1]
     second = lax.broadcasted_iota(jnp.int32, (1, row_len), 1) >= row_len // 2
     for q in range(SIDE):
         for j in range(SIDE):
-            other = lax.rem(cent_pos + SHIFTS[j], SIDE)
+            other = cent_pos ^ SHIFTS[j]
             block = jnp.where(core == 0, q * SIDE + other, other * SIDE + q)
             hits = []
             for b in range(list_ref.shape[0]):
@@ -107,40 +121,47 @@
             stat_ref[q * SIDE + j : q * SIDE + j + 1, :] = jnp.where(second, hits[1], hits[0])
 
 
-def first_score_kernel(scale, pos_ref, list_ref, *refs):
+def near_score_kernel(scale, pos_ref, list_ref, *refs):
     allow_rows(pos_ref, list_ref, refs[-1])
-    score_kernel(scale, 1, 0, *refs, base=SIDE * SIDE)
-
-
-def score_kernel(scale, n_rows, extra, *refs, base=0):
-    rows, cents = refs[:n_rows], refs[n_rows : n_rows + SIDE]
-    before = refs[n_rows + SIDE : n_rows + SIDE + extra]
-    exps = refs[n_rows + SIDE + extra : n_rows + 2 * SIDE + extra]
-    stat_ref = refs[n_rows + 2 * SIDE + extra]
+    n = len(NEAR)
+    rows, cents, exps = refs[:n], refs[n : n + SIDE], refs[n + SIDE : -1]
+    score(scale, NEAR, rows, cents, exps, refs[-1])
+
+
+def far_score_kernel(scale, *refs):
+    n = len(FAR)
+    rows, cents, before_ref = refs[:n], refs[n : n + SIDE], refs[n + SIDE]
+    exps, stat_ref = refs[n + SIDE + 1 : -1], refs[-1]
+    stat_ref[...] = before_ref[...]
+    score(scale, FAR, rows, cents, exps, stat_ref)
+
+
+def lanes_of(half, row_ref):
+    start = row_ref.shape[0] if half == 1 else 0
+    return slice(start, start + row_ref.shape[0])
+
+
+def score(scale, pieces, rows, cents, exps, stat_ref):
     width = rows[0].shape[1]
-    for ref in before:
-        stat_ref[base : base + ref.shape[0], :] = ref[...]
-        base += ref.shape[0]
     for j in range(SIDE):
-        half = read_tail(cents[j], width)
-        start = 0
-        for row_ref in rows:
-            stop = start + row_ref.shape[0]
+        half_norm = read_tail(cents[j], width)
+        for i, (t, half) in enumerate(pieces):
+            line = SIDE * SIDE + 2 * SIDE * t + j
+            lanes = lanes_of(half, rows[i])
             dots = lax.dot_general(
                 cents[j][:, :width],
-                row_ref[...],
+                rows[i][...],
                 (((1,), (1,)), ((), ())),
                 preferred_element_type=jnp.float32,
             )
-            logits = (dots - half) * scale
+            logits = (dots - half_norm) * scale
             peak = jnp.max(logits, axis=0, keepdims=True)
             exp_values = jnp.exp(logits - peak)
-            exps[j][:, start:stop] = exp_values
-            stat_ref[base + j : base + j + 1, start:stop] = peak
-            stat_ref[base + SIDE + j : base + SIDE + j + 1, start:stop] = jnp.sum(
+            exps[i * SIDE + j][...] = exp_values
+            stat_ref[line : line + 1, lanes] = peak
+            stat_ref[line + SIDE : line + SIDE + 1, lanes] = jnp.sum(
                 exp_values, axis=0, keepdims=True
             )
-            start = stop
 
 
 def norm_kernel(pos_ref, all_ref, own_ref, scale_ref, log_ref, sum_ref):
@@ -159,7 +180,7 @@
         allow = allowed(r)
         peaks, totals = [], []
         for q in range(SIDE):
-            peak, total = stat_rows(all_ref.at[q], SHIFTS.index((r - q) % SIDE))
+            peak, total = stat_rows(all_ref.at[q], SHIFTS.index(r ^ q))
             peaks.append(peak)
             totals.append(total)
         peak = jnp.concatenate(peaks, axis=0)
@@ -170,7 +191,7 @@
     row_sum = logs[0] + logs[1] + logs[2] + logs[3]
     sum_ref[...] = jnp.broadcast_to(jnp.sum(row_sum, axis=1, keepdims=True), sum_ref.shape)
     for t in range(SIDE):
-        place = lax.rem(me + SHIFTS[t], SIDE)
+        place = me ^ SHIFTS[t]
         log_t = jnp.zeros_like(logs[0])
         allow_t = jnp.zeros((SIDE, log_t.shape[1]), jnp.float32)
         for r in range(SIDE):
@@ -190,31 +211,25 @@
 
 def weighted(j, scale_ref, exps, rows):
     total, lanes = None, None
-    for t in range(SIDE):
-        weights = exps[t][...] * scale_ref[t * SIDE + j : t * SIDE + j + 1, :]
+    for i, (t, half) in enumerate(NEAR + FAR):
+        line = t * SIDE + j
+        weights = exps[i * SIDE + j][...] * scale_ref[line : line + 1, lanes_of(half, rows[i])]
         for start in range(0, weights.shape[1], PAD):
             piece = weights[:, start : start + PAD]
             lanes = piece if lanes is None else lanes + piece
-        rounded = weights.astype(jnp.bfloat16)
-        start = 0
-        for row_ref in rows[t]:
-            stop = start + row_ref.shape[0]
-            term = jnp.dot(
-                rounded[:, start:stop], row_ref[...], preferred_element_type=jnp.float32
-            )
-            total = term if total is None else total + term
-            start = stop
+        term = jnp.dot(
+            weights.astype(jnp.bfloat16), rows[i][...], preferred_element_type=jnp.float32
+        )
+        total = term if total is None else total + term
     return total, jnp.sum(lanes, axis=1, keepdims=True)
 
 
 def sums_kernel(scale_ref, *refs):
-    n_rows = SIDE + 1
-    flat, row_refs = refs[: SIDE * SIDE], refs[SIDE * SIDE : SIDE * SIDE + n_rows]
-    outs = refs[SIDE * SIDE + n_rows :]
-    rows = [[row_refs[0]], [row_refs[1]], [row_refs[2]], [row_refs[3], row_refs[4]]]
-    width = row_refs[0].shape[1]
+    n_rows = len(NEAR) + len(FAR)
+    exps, rows = refs[: n_rows * SIDE], refs[n_rows * SIDE : n_rows * (SIDE + 1)]
+    outs = refs[n_rows * (SIDE + 1) :]
+    width = rows[0].shape[1]
     for j in range(SIDE - 1, -1, -1):
-        exps = [flat[t * SIDE + j] for t in range(SIDE)]
         total, counts = weighted(j, scale_ref, exps, rows)
         if j == 0:
             outs[0][...] = total
@@ -265,38 +280,53 @@
 
     packed = call(pack_kernel, shape((BLK, width + PAD), bf16), 1, 8, nbytes=2 << 20)(centroids)
     cents = [packed] + [bulk(packed, cent_pairs(planes, SHIFTS[t])) for t in range(1, SIDE)]
-    near = bulk(embeddings, row_pairs(planes, 1))
-    back = bulk(embeddings, row_pairs(planes, SIDE - 1))
     half = row_len // 2
-    far = [bulk(near[:half], row_pairs(planes, 1)), bulk(back[half:], row_pairs(planes, SIDE - 1))]
-    rows = [[embeddings], [near], [back], far]
+    halves = pl.pallas_call(
+        split_kernel,
+        name="split",
+        out_shape=[shape((half, width), bf16)] * 2,
+        in_specs=[pl.BlockSpec(memory_space=pl.ANY)],
+        out_specs=[pl.BlockSpec(memory_space=pltpu.VMEM)] * 2,
+        scratch_shapes=[pltpu.SemaphoreType.DMA((2,))],
+        cost_estimate=pl.CostEstimate(flops=0, bytes_accessed=2 << 20, transcendentals=0),
+        compiler_params=pltpu.CompilerParams(vmem_limit_bytes=4 << 20),
+    )(embeddings)
+    piece = {(0, None): embeddings}
+    for t in (1, 2):
+        for h in (0, 1):
+            piece[t, h] = bulk(halves[h], row_pairs(planes, SHIFTS[t]))
+    piece[3, 1] = bulk(piece[1, 1], row_pairs(planes, SHIFTS[2]))
+    piece[3, 0] = bulk(piece[2, 0], row_pairs(planes, SHIFTS[1]))
+    near = [piece[key] for key in NEAR]
+    far = [piece[key] for key in FAR]
+    rows = near + far
 
     pos = jnp.stack([row_pos, core, cent_pos]).astype(jnp.int32)
-    exps, stats = [], []
     pair_flops = 2 * row_len * SIDE * BLK * width
-    for t in range(SIDE):
-        extra = stats if t == SIDE - 1 else []
-        stat_rows = 2 * SIDE + sum(part.shape[0] for part in extra)
-        scalars = (pos, candidates) if t == 0 else ()
-        if t == 0:
-            stat_rows += SIDE * SIDE
-            kernel = functools.partial(first_score_kernel, 1.0 / width**0.5)
-        else:
-            kernel = functools.partial(
-                score_kernel, 1.0 / width**0.5, len(rows[t]), len(extra)
-            )
-        *exp_values, stat = call(
-            kernel,
-            [shape((BLK, row_len), f32)] * SIDE + [shape((stat_rows, row_len), f32)],
-            len(scalars) + len(rows[t]) + SIDE + len(extra),
-            12,
-            flops=pair_flops,
-            nbytes=6 << 20,
-            smem=len(scalars),
-        )(*scalars, *rows[t], *cents, *extra)
-        exps.append(exp_values)
-        stats.append(stat)
-    own_stats = stats[-1]
+    factor = 1.0 / width**0.5
+    stat_shape = shape((SIDE * SIDE + 2 * SIDE * SIDE, row_len), f32)
+
+    def exp_shapes(values):
+        return [shape((BLK, value.shape[0]), f32) for value in values for _ in range(SIDE)]
+
+    *near_exps, near_stats = call(
+        functools.partial(near_score_kernel, factor),
+        exp_shapes(near) + [stat_shape],
+        2 + len(near) + SIDE,
+        16,
+        flops=3 * pair_flops,
+        nbytes=14 << 20,
+        smem=2,
+    )(pos, candidates, *near, *cents)
+    *far_exps, own_stats = call(
+        functools.partial(far_score_kernel, factor),
+        exp_shapes(far) + [stat_shape],
+        len(far) + SIDE + 1,
+        12,
+        flops=pair_flops,
+        nbytes=6 << 20,
+    )(*far, *cents, near_stats)
+    exps = near_exps + far_exps
     all_stats = lax.all_gather(own_stats, AXES, axis_index_groups=row_lines(planes))
     n_cover = planes * CORES * SIDE
     scale, log_rows, line_sum = call(
@@ -306,23 +336,23 @@
         4,
         nbytes=1 << 20,
         smem=1,
-    )(pos, all_stats, own_stats)
+    )(row_pos.reshape(1).astype(jnp.int32), all_stats, own_stats)
 
     total, *sent, counts = call(
         sums_kernel,
         [shape((BLK, width), f32)]
         + [shape((BLK, width + PAD), bf16)] * (SIDE - 1)
         + [shape((BLK, PAD), f32)],
-        2 + SIDE * SIDE + SIDE,
+        1 + len(exps) + len(rows),
         24,
         flops=SIDE * pair_flops,
         nbytes=16 << 20,
-    )(scale, *[value for values in exps for value in values], *[part for parts in rows for part in parts])
+    )(scale, *exps, *rows)
     line_sum, total = lax.optimization_barrier((line_sum, total))
     cover_sums = lax.all_to_all(
         line_sum, AXES, 0, 0, tiled=True, axis_index_groups=line_covers(planes)
     )
-    received = [bulk(sent[j - 1], cent_pairs(planes, -SHIFTS[j] % SIDE)) for j in (3, 1, 2)]
+    received = [bulk(sent[j - 1], cent_pairs(planes, SHIFTS[j])) for j in (3, 2, 1)]
     tile = BLK // 2
     spec = lambda cols: pl.BlockSpec((tile, cols), lambda i: (i, 0))
     new_centroids = pl.pallas_call(

time: 122 us -> 121 us (level)
  Pallas kernels: 23.7 us -> 21.3 us
    ppermute x10 -> x12, starting transfers between devices: 39.1 us -> 35.9 us  [bulk(): return lax.ppermute(value, AXES, pairs)]
    all_to_all x1, starting transfers between devices: 22.3 us -> 25.2 us  [step(): lax.all_to_all(line_sum, AXES, 0, 0, tiled=True, axis_index_groups=line_c...]
    unnamed x14 -> x16, local copies, waits for them, and re-layouts: 2.47 us -> 5.1 us
    pallas_call x4 -> x3, Pallas kernels: 12.9 us -> 10.4 us  [the longest x1 6.24 us: step(): call(functools.partial(near_score_kernel, factor), exp_shapes(near) + [st...]
    slice x2 -> x0, local copies, waits for them, and re-layouts: 1.7 us -> none  [the longest x1 0.87 us: step(): near[:half]]
    ppermute x10 -> x12, waiting for transfers between devices: 6.45 us -> 7.04 us  [bulk(): return lax.ppermute(value, AXES, pairs)]
  transfers between devices with their start and end apart: 11 -> 13, of which waited for: 4 -> 5; matrix products, arithmetic and copies ran while one was open for 1% -> 0% of each run, Pallas kernels for 10% -> 7%
where the time goes in v2:
time: 121 us; the launch traced here: 120 us
  starting transfers between devices  61.1 us (50%)
  Pallas kernels  21.3 us (18%)
  waiting for transfers between devices  18.9 us (16%)
  blocking collectives  10.5 us (9%)
  local copies, waits for them, and re-layouts  5.1 us (4%)
  between operations  2.65 us (2%)
    ppermute x12, starting transfers between devices, bulk(): return lax.ppermute(value, AXES, pairs)  35.9 us
    all_to_all x1, starting transfers between devices, step(): lax.all_to_all(line_sum, AXES, 0, 0, tiled=True, axis_index_groups=line_c...  25.2 us
    all_to_all x1, waiting for transfers between devices, step(): lax.all_to_all(line_sum, AXES, 0, 0, tiled=True, axis_index_groups=line_c...  11.9 us
    all_gather x1, blocking collectives, step(): lax.all_gather(own_stats, AXES, axis_index_groups=row_lines(planes))  10.5 us
    pallas_call x1, Pallas kernels, step(): call(sums_kernel, [shape((BLK, width), f32)] + [shape((BLK, width + PAD),...  7.55 us
    ppermute x12, waiting for transfers between devices, bulk(): return lax.ppermute(value, AXES, pairs)  7.04 us
    pallas_call x1, Pallas kernels, step(): call(functools.partial(near_score_kernel, factor), exp_shapes(near) + [st...  6.24 us
    unnamed x16, local copies, waits for them, and re-layouts  5.1 us
  transfers between devices with their start and end apart: 13, of which 5 were waited for; matrix products, arithmetic and copies ran while one was open for 0% of the time, Pallas kernels for 7%

profile of v2, /device:TPU:1, one launch (start us, length us, event | category | flops | bytes accessed | tf_op | source)
XLA Modules:
  0.0 120.2 jit_solution(11719480072453532852)
XLA Ops:
  0.7 1.3 %copy-done.1 = bf16[512,1024]{1,0:T(8,128)(2,1)S(1)} copy-done((bf16[512,1024]{1,0:T(8,128)(2,1)S(1)}, bf16[512,1024]{1,0:T(8,128)(2,1)}, u32[]{:S(2)}) %copy-start.1) | copy-done | bytes 1048600
  2.0 1.1 split.1
  3.1 5.6 %collective-permute-start.6 = (bf16[256,1024]{1,0:T(8,128)(2,1)}, bf16[256,1024]{1,0:T(8,128)(2,1)}, u32[]{:S(2)}, u32[]{:S(2)}) collective-permute-start(bf16[256,1024]{1,0:T(8,128)(2,1)} %get-tuple-element.47), channel_id=1, source_target_pairs={{12,0},{13,1},{14,2},{15,3},{8,4},{9,5},{10,6},{11,7},{4,8},{5,9},... | collective-permute-start | bytes 1572872 | tf_op jit(solution)/shard_map/ppermute | solution.py:267
  8.7 1.9 %collective-permute-start.5 = (bf16[256,1024]{1,0:T(8,128)(2,1)}, bf16[256,1024]{1,0:T(8,128)(2,1)}, u32[]{:S(2)}, u32[]{:S(2)}) collective-permute-start(bf16[256,1024]{1,0:T(8,128)(2,1)} %get-tuple-element.48), channel_id=1, source_target_pairs={{4,0},{5,1},{6,2},{7,3},{0,4},{1,5},{2,6},{3,7},{12,8},{13,9},{14,... | collective-permute-start | bytes 1572872 | tf_op jit(solution)/shard_map/ppermute | solution.py:267
  10.8 4.7 %collective-permute-start.4 = (bf16[256,1152]{1,0:T(8,128)(2,1)S(1)}, bf16[256,1152]{1,0:T(8,128)(2,1)S(1)}, u32[]{:S(2)}, u32[]{:S(2)}) collective-permute-start(bf16[256,1152]{1,0:T(8,128)(2,1)S(1)} %shard_map.58.refs_5_.refs_2_), channel_id=1, source_target_pairs={{2,0},{3,1},{0,2},{1,3},{6,4},{7,5},{4,6},{5,7},{10,8},{11,9},{8,1... | collective-permute-start | bytes 1769480 | tf_op jit(solution)/shard_map/ppermute | solution.py:267
  15.5 2.8 %collective-permute-start.3 = (bf16[256,1152]{1,0:T(8,128)(2,1)S(1)}, bf16[256,1152]{1,0:T(8,128)(2,1)S(1)}, u32[]{:S(2)}, u32[]{:S(2)}) collective-permute-start(bf16[256,1152]{1,0:T(8,128)(2,1)S(1)} %shard_map.58.refs_5_.refs_2_), channel_id=1, source_target_pairs={{3,0},{2,1},{1,2},{0,3},{7,4},{6,5},{5,6},{4,7},{11,8},{10,9},{9,1... | collective-permute-start | bytes 1769480 | tf_op jit(solution)/shard_map/ppermute | solution.py:267
  18.2 1.9 %collective-permute-start.2 = (bf16[256,1152]{1,0:T(8,128)(2,1)S(1)}, bf16[256,1152]{1,0:T(8,128)(2,1)}, u32[]{:S(2)}, u32[]{:S(2)}) collective-permute-start(bf16[256,1152]{1,0:T(8,128)(2,1)S(1)} %shard_map.58.refs_5_.refs_2_), channel_id=1, source_target_pairs={{1,0},{0,1},{3,2},{2,3},{5,4},{4,5},{7,6},{6,7},{9,8},{8,9},{11,10... | collective-permute-start | bytes 1769480 | tf_op jit(solution)/shard_map/ppermute | solution.py:267
  20.2 3.4 %collective-permute-start.7 = (bf16[256,1024]{1,0:T(8,128)(2,1)}, bf16[256,1024]{1,0:T(8,128)(2,1)}, u32[]{:S(2)}, u32[]{:S(2)}) collective-permute-start(bf16[256,1024]{1,0:T(8,128)(2,1)} %collective-permute-done.6.refs_2_.refs_30_), channel_id=1, source_target_pairs={{4,0},{5,1},{6,2},{7,3},{0,4},{1,5},{2,6},{3,7},{12,8},{13,9},{14,... | collective-permute-start | bytes 1572872 | tf_op jit(solution)/shard_map/ppermute | solution.py:267
  23.6 1.9 %collective-permute-start.8 = (bf16[256,1024]{1,0:T(8,128)(2,1)}, bf16[256,1024]{1,0:T(8,128)(2,1)}, u32[]{:S(2)}, u32[]{:S(2)}) collective-permute-start(bf16[256,1024]{1,0:T(8,128)(2,1)} %collective-permute-done.5.refs_1_.refs_29_), channel_id=1, source_target_pairs={{12,0},{13,1},{14,2},{15,3},{8,4},{9,5},{10,6},{11,7},{4,8},{5,9},... | collective-permute-start | bytes 1572872 | tf_op jit(solution)/shard_map/ppermute | solution.py:267
  25.5 1.3 %collective-permute-done.4.refs_8_.refs_5_ = bf16[256,1152]{1,0:T(8,128)(2,1)S(1)} collective-permute-done((bf16[256,1152]{1,0:T(8,128)(2,1)S(1)}, bf16[256,1152]{1,0:T(8,128)(2,1)S(1)}, u32[]{:S(2)}, u32[]{:S(2)}) %collective-permute-start.4) | collective-permute-done | bytes 589856 | tf_op jit(solution)/shard_map/ppermute | solution.py:267
  27.6 2.7 %collective-permute-start = (bf16[256,1024]{1,0:T(8,128)(2,1)}, bf16[256,1024]{1,0:T(8,128)(2,1)}, u32[]{:S(2)}, u32[]{:S(2)}) collective-permute-start(bf16[256,1024]{1,0:T(8,128)(2,1)} %get-tuple-element.47), channel_id=1, source_target_pairs={{4,0},{5,1},{6,2},{7,3},{0,4},{1,5},{2,6},{3,7},{12,8},{13,9},{14,... | collective-permute-start | bytes 1572872 | tf_op jit(solution)/shard_map/ppermute | solution.py:267
  30.3 4.4 %collective-permute-done.3.refs_7_.refs_4_ = bf16[256,1152]{1,0:T(8,128)(2,1)S(1)} collective-permute-done((bf16[256,1152]{1,0:T(8,128)(2,1)S(1)}, bf16[256,1152]{1,0:T(8,128)(2,1)S(1)}, u32[]{:S(2)}, u32[]{:S(2)}) %collective-permute-start.3) | collective-permute-done | bytes 589856 | tf_op jit(solution)/shard_map/ppermute | solution.py:267
  35.6 1.9 %collective-permute-start.1 = (bf16[256,1024]{1,0:T(8,128)(2,1)}, bf16[256,1024]{1,0:T(8,128)(2,1)}, u32[]{:S(2)}, u32[]{:S(2)}) collective-permute-start(bf16[256,1024]{1,0:T(8,128)(2,1)} %get-tuple-element.48), channel_id=1, source_target_pairs={{12,0},{13,1},{14,2},{15,3},{8,4},{9,5},{10,6},{11,7},{4,8},{5,9},... | collective-permute-start | bytes 1572872 | tf_op jit(solution)/shard_map/ppermute | solution.py:267
  37.7 1.1 collective-permute-done.8.refs_4_.refs_32_
  40.9 6.2 %shard_map.59 = (f32[256,512]{1,0:T(8,128)S(1)}, f32[256,512]{1,0:T(8,128)S(1)}, f32[256,512]{1,0:T(8,128)S(1)}, f32[256,512]{1,0:T(8,128)S(1)}, f32[256,256]{1,...) custom-call(s32[3]{0:T(128)S(1)} %pad_add_fusion.pos_ref, ...), custom_call_target="tpu_custom_call" | custom-call | flops 3221225472 | bytes 14680064 | tf_op jit(solution)/shard_map/pallas_call | solution.py:312
  47.3 3.1 %shard_map.60 = (f32[256,256]{1,0:T(8,128)S(1)}, f32[256,256]{1,0:T(8,128)S(1)}, f32[256,256]{1,0:T(8,128)S(1)}, f32[256,256]{1,0:T(8,128)S(1)}, f32[256,256]{1,...) custom-call(bf16[256,1024]{1,0:T(8,128)(2,1)} %collective-permute-do, ...), custom_call_target="tpu_custom_call" | custom-call | flops 1073741824 | bytes 6291456 | tf_op jit(solution)/shard_map/pallas_call | solution.py:321
  50.4 10.5 %all-gather = f32[192,512]{1,0:T(8,128)S(1)} all-gather(f32[48,512]{1,0:T(8,128)S(1)} %get-tuple-element.50.own_ref), channel_id=2, replica_groups={{0,4,8,12},{1,5,9,13},{2,6,10,14},{3,7,11,15},{16,17,18,19},{20,21,22,2..., dimensions={0}, use_global_device_ids=true | all-gather | bytes 491520 | tf_op jit(solution)/shard_map/all_gather | solution.py:330
  61.7 7.5 %shard_map.62 = (f32[256,1024]{1,0:T(8,128)S(1)}, bf16[256,1152]{1,0:T(8,128)(2,1)}, bf16[256,1152]{1,0:T(8,128)(2,1)}, bf16[256,1152]{1,0:T(8,128)(2,1)}, f32[256,128]{1,0:T(8,128)S(1)}) custom-call(f32[16,512]{1,0:T(8,128)S(1)} %get-tuple-element.52.scale_ref, f32[256,512]{1,0:T(8,128)S(1)} %get-tuple-element.53.refs_0_, ...), custom_call_target="tpu_custom_call" | custom-call | flops 4294967296 | bytes 16777216 | tf_op jit(solution)/shard_map/pallas_call | solution.py:341
  69.3 5.2 %collective-permute-start.9 = (bf16[256,1152]{1,0:T(8,128)(2,1)}, bf16[256,1152]{1,0:T(8,128)(2,1)S(1)}, u32[]{:S(2)}, u32[]{:S(2)}) collective-permute-start(bf16[256,1152]{1,0:T(8,128)(2,1)} %get-tuple-element.84), channel_id=1, source_target_pairs={{2,0},{3,1},{0,2},{1,3},{6,4},{7,5},{4,6},{5,7},{10,8},{11,9},{8,1... | collective-permute-start | bytes 1769480 | tf_op jit(solution)/shard_map/ppermute | solution.py:267
  74.5 1.9 %collective-permute-start.10 = (bf16[256,1152]{1,0:T(8,128)(2,1)}, bf16[256,1152]{1,0:T(8,128)(2,1)S(1)}, u32[]{:S(2)}, u32[]{:S(2)}) collective-permute-start(bf16[256,1152]{1,0:T(8,128)(2,1)} %get-tuple-element.85), channel_id=1, source_target_pairs={{3,0},{2,1},{1,2},{0,3},{7,4},{6,5},{5,6},{4,7},{11,8},{10,9},{9,1... | collective-permute-start | bytes 1769480 | tf_op jit(solution)/shard_map/ppermute | solution.py:267
  76.5 1.9 %collective-permute-start.11 = (bf16[256,1152]{1,0:T(8,128)(2,1)}, bf16[256,1152]{1,0:T(8,128)(2,1)}, u32[]{:S(2)}, u32[]{:S(2)}) collective-permute-start(bf16[256,1152]{1,0:T(8,128)(2,1)} %get-tuple-element.86), channel_id=1, source_target_pairs={{1,0},{0,1},{3,2},{2,3},{5,4},{4,5},{7,6},{6,7},{9,8},{8,9},{11,10... | collective-permute-start | bytes 1769480 | tf_op jit(solution)/shard_map/ppermute | solution.py:267
  78.4 25.2 %all-to-all-start = ((f32[128,1,128]{2,1,0:T(1,128)}), f32[128,1,128]{2,1,0:T(1,128)S(1)}, u32[]{:S(2)}, u32[]{:S(2)}) async-start(f32[128,1,128]{2,1,0:T(1,128)} %bitcast.5), calls=%async_computation | async-start | bytes 131072 | tf_op jit(solution)/shard_map/all_to_all | solution.py:352
  103.7 2.3 %final.1 = f32[256,1024]{1,0:T(8,128)} custom-call(f32[256,1024]{1,0:T(8,128)S(1)} %get-tuple-element.82.total_ref, f32[256,128]{1,0:T(8,128)S(1)} %get-tuple-element.83.count_ref, bf16[256,1152]{1,0:T(8,128)(2,1)S(1)} %collective-permute-done.9.a_ref, bf16[256,1152]{1,0:T(8,128)(2,1)S(1)} %collective-permute-done.10.b_ref, ...), custom_call_target="tpu_custom_call" | custom-call | bytes 5242880 | tf_op jit(solution)/shard_map/final/pallas_call | solution.py:358
  106.0 11.9 %all-to-all-done = f32[128,1,128]{2,1,0:T(1,128)S(1)} async-done(((f32[128,1,128]{2,1,0:T(1,128)}), f32[128,1,128]{2,1,0:T(1,128)S(1)}, u32[]{:S(2)}, u32[]{:S(2)}) %all-to-all-start) | async-done | bytes 65568 | tf_op jit(solution)/shard_map/all_to_all | solution.py:352
  (28 shorter events, 5.7 us)
Async XLA Ops:
  0.6 10.0 %copy-start = (f32[256,1024]{1,0:T(8,128)S(1)}, f32[256,1024]{1,0:T(8,128)}, u32[]{:S(2)}) copy-start(f32[256,1024]{1,0:T(8,128)} %old_ref.1) | copy-start | bytes 3145732
  0.6 1.3 %copy-start.1 = (bf16[512,1024]{1,0:T(8,128)(2,1)S(1)}, bf16[512,1024]{1,0:T(8,128)(2,1)}, u32[]{:S(2)}) copy-start(bf16[512,1024]{1,0:T(8,128)(2,1)} %refs_28_.1) | copy-start | bytes 3145732
  3.1 35.7 %copy-start.2 = (bf16[512,1024]{1,0:T(8,128)(2,1)S(1)}, bf16[512,1024]{1,0:T(8,128)(2,1)}, u32[]{:S(2)}) copy-start(bf16[512,1024]{1,0:T(8,128)(2,1)} %refs_28_.1) | copy-start | bytes 3145732
  3.1 17.1 %collective-permute-start.6 = (bf16[256,1024]{1,0:T(8,128)(2,1)}, bf16[256,1024]{1,0:T(8,128)(2,1)}, u32[]{:S(2)}, u32[]{:S(2)}) collective-permute-start(bf16[256,1024]{1,0:T(8,128)(2,1)} %get-tuple-element.47), channel_id=1, source_target_pairs={{12,0},{13,1},{14,2},{15,3},{8,4},{9,5},{10,6},{11,7},{4,8},{5,9},... | collective-permute-start | bytes 1572872 | tf_op jit(solution)/shard_map/ppermute | solution.py:267
  8.7 14.9 %collective-permute-start.5 = (bf16[256,1024]{1,0:T(8,128)(2,1)}, bf16[256,1024]{1,0:T(8,128)(2,1)}, u32[]{:S(2)}, u32[]{:S(2)}) collective-permute-start(bf16[256,1024]{1,0:T(8,128)(2,1)} %get-tuple-element.48), channel_id=1, source_target_pairs={{4,0},{5,1},{6,2},{7,3},{0,4},{1,5},{2,6},{3,7},{12,8},{13,9},{14,... | collective-permute-start | bytes 1572872 | tf_op jit(solution)/shard_map/ppermute | solution.py:267
  10.8 16.0 %collective-permute-start.4 = (bf16[256,1152]{1,0:T(8,128)(2,1)S(1)}, bf16[256,1152]{1,0:T(8,128)(2,1)S(1)}, u32[]{:S(2)}, u32[]{:S(2)}) collective-permute-start(bf16[256,1152]{1,0:T(8,128)(2,1)S(1)} %shard_map.58.refs_5_.refs_2_), channel_id=1, source_target_pairs={{2,0},{3,1},{0,2},{1,3},{6,4},{7,5},{4,6},{5,7},{10,8},{11,9},{8,1... | collective-permute-start | bytes 1769480 | tf_op jit(solution)/shard_map/ppermute | solution.py:267
  15.5 19.3 %collective-permute-start.3 = (bf16[256,1152]{1,0:T(8,128)(2,1)S(1)}, bf16[256,1152]{1,0:T(8,128)(2,1)S(1)}, u32[]{:S(2)}, u32[]{:S(2)}) collective-permute-start(bf16[256,1152]{1,0:T(8,128)(2,1)S(1)} %shard_map.58.refs_5_.refs_2_), channel_id=1, source_target_pairs={{3,0},{2,1},{1,2},{0,3},{7,4},{6,5},{5,6},{4,7},{11,8},{10,9},{9,1... | collective-permute-start | bytes 1769480 | tf_op jit(solution)/shard_map/ppermute | solution.py:267
  18.2 19.4 %collective-permute-start.2 = (bf16[256,1152]{1,0:T(8,128)(2,1)S(1)}, bf16[256,1152]{1,0:T(8,128)(2,1)}, u32[]{:S(2)}, u32[]{:S(2)}) collective-permute-start(bf16[256,1152]{1,0:T(8,128)(2,1)S(1)} %shard_map.58.refs_5_.refs_2_), channel_id=1, source_target_pairs={{1,0},{0,1},{3,2},{2,3},{5,4},{4,5},{7,6},{6,7},{9,8},{8,9},{11,10... | collective-permute-start | bytes 1769480 | tf_op jit(solution)/shard_map/ppermute | solution.py:267
  20.2 17.5 %collective-permute-start.7 = (bf16[256,1024]{1,0:T(8,128)(2,1)}, bf16[256,1024]{1,0:T(8,128)(2,1)}, u32[]{:S(2)}, u32[]{:S(2)}) collective-permute-start(bf16[256,1024]{1,0:T(8,128)(2,1)} %collective-permute-done.6.refs_2_.refs_30_), channel_id=1, source_target_pairs={{4,0},{5,1},{6,2},{7,3},{0,4},{1,5},{2,6},{3,7},{12,8},{13,9},{14,... | collective-permute-start | bytes 1572872 | tf_op jit(solution)/shard_map/ppermute | solution.py:267
  23.6 15.2 %collective-permute-start.8 = (bf16[256,1024]{1,0:T(8,128)(2,1)}, bf16[256,1024]{1,0:T(8,128)(2,1)}, u32[]{:S(2)}, u32[]{:S(2)}) collective-permute-start(bf16[256,1024]{1,0:T(8,128)(2,1)} %collective-permute-done.5.refs_1_.refs_29_), channel_id=1, source_target_pairs={{12,0},{13,1},{14,2},{15,3},{8,4},{9,5},{10,6},{11,7},{4,8},{5,9},... | collective-permute-start | bytes 1572872 | tf_op jit(solution)/shard_map/ppermute | solution.py:267
  26.8 0.8 copy-start.3
  27.6 19.5 %collective-permute-start = (bf16[256,1024]{1,0:T(8,128)(2,1)}, bf16[256,1024]{1,0:T(8,128)(2,1)}, u32[]{:S(2)}, u32[]{:S(2)}) collective-permute-start(bf16[256,1024]{1,0:T(8,128)(2,1)} %get-tuple-element.47), channel_id=1, source_target_pairs={{4,0},{5,1},{6,2},{7,3},{0,4},{1,5},{2,6},{3,7},{12,8},{13,9},{14,... | collective-permute-start | bytes 1572872 | tf_op jit(solution)/shard_map/ppermute | solution.py:267
  34.8 0.8 copy-start.5
  35.6 11.7 %collective-permute-start.1 = (bf16[256,1024]{1,0:T(8,128)(2,1)}, bf16[256,1024]{1,0:T(8,128)(2,1)}, u32[]{:S(2)}, u32[]{:S(2)}) collective-permute-start(bf16[256,1024]{1,0:T(8,128)(2,1)} %get-tuple-element.48), channel_id=1, source_target_pairs={{12,0},{13,1},{14,2},{15,3},{8,4},{9,5},{10,6},{11,7},{4,8},{5,9},... | collective-permute-start | bytes 1572872 | tf_op jit(solution)/shard_map/ppermute | solution.py:267
  37.6 1.2 copy-start.7
  38.7 1.1 copy-start.4
  39.8 1.1 copy-start.6
  69.3 34.4 %collective-permute-start.9 = (bf16[256,1152]{1,0:T(8,128)(2,1)}, bf16[256,1152]{1,0:T(8,128)(2,1)S(1)}, u32[]{:S(2)}, u32[]{:S(2)}) collective-permute-start(bf16[256,1152]{1,0:T(8,128)(2,1)} %get-tuple-element.84), channel_id=1, source_target_pairs={{2,0},{3,1},{0,2},{1,3},{6,4},{7,5},{4,6},{5,7},{10,8},{11,9},{8,1... | collective-permute-start | bytes 1769480 | tf_op jit(solution)/shard_map/ppermute | solution.py:267
  74.5 29.1 %collective-permute-start.10 = (bf16[256,1152]{1,0:T(8,128)(2,1)}, bf16[256,1152]{1,0:T(8,128)(2,1)S(1)}, u32[]{:S(2)}, u32[]{:S(2)}) collective-permute-start(bf16[256,1152]{1,0:T(8,128)(2,1)} %get-tuple-element.85), channel_id=1, source_target_pairs={{3,0},{2,1},{1,2},{0,3},{7,4},{6,5},{5,6},{4,7},{11,8},{10,9},{9,1... | collective-permute-start | bytes 1769480 | tf_op jit(solution)/shard_map/ppermute | solution.py:267
  76.5 27.2 %collective-permute-start.11 = (bf16[256,1152]{1,0:T(8,128)(2,1)}, bf16[256,1152]{1,0:T(8,128)(2,1)}, u32[]{:S(2)}, u32[]{:S(2)}) collective-permute-start(bf16[256,1152]{1,0:T(8,128)(2,1)} %get-tuple-element.86), channel_id=1, source_target_pairs={{1,0},{0,1},{3,2},{2,3},{5,4},{4,5},{7,6},{6,7},{9,8},{8,9},{11,10... | collective-permute-start | bytes 1769480 | tf_op jit(solution)/shard_map/ppermute | solution.py:267
  78.4 39.5 %all-to-all-start = ((f32[128,1,128]{2,1,0:T(1,128)}), f32[128,1,128]{2,1,0:T(1,128)S(1)}, u32[]{:S(2)}, u32[]{:S(2)}) async-start(f32[128,1,128]{2,1,0:T(1,128)} %bitcast.5), calls=%async_computation | async-start | bytes 131072 | tf_op jit(solution)/shard_map/all_to_all | solution.py:352

commit v3 on v2

--- a/solution.py
+++ b/solution.py
@@ -49,6 +49,15 @@
     ]
 
 
+def cent_lines(planes):
+    return [
+        [line_device(z, c, r, k) for k in range(SIDE)]
+        for z in range(planes)
+        for c in range(CORES)
+        for r in range(SIDE)
+    ]
+
+
 def row_lines(planes):
     return [
         [line_device(z, c, r, k) for r in range(SIDE)]
@@ -88,8 +97,11 @@
 def pack_kernel(cent_ref, out_ref):
     width = cent_ref.shape[1]
     values = cent_ref[...]
-    out_ref[:, :width] = values.astype(jnp.bfloat16)
-    out_ref[:, width:] = tail_lanes(0.5 * jnp.sum(values * values, axis=1, keepdims=True))
+    rounded = values.astype(jnp.bfloat16)
+    tail = tail_lanes(0.5 * jnp.sum(values * values, axis=1, keepdims=True))
+    for j in range(SIDE):
+        out_ref[j, :, :width] = rounded
+        out_ref[j, :, width:] = tail
 
 
 def split_kernel(row_ref, first_ref, second_ref, sems):
@@ -105,13 +117,12 @@
 
 
 def allow_rows(pos_ref, list_ref, stat_ref):
-    core, cent_pos = pos_ref[1], pos_ref[2]
+    core = pos_ref[1]
     row_len = stat_ref.shape[1]
     second = lax.broadcasted_iota(jnp.int32, (1, row_len), 1) >= row_len // 2
     for q in range(SIDE):
         for j in range(SIDE):
-            other = cent_pos ^ SHIFTS[j]
-            block = jnp.where(core == 0, q * SIDE + other, other * SIDE + q)
+            block = jnp.where(core == 0, q * SIDE + j, j * SIDE + q)
             hits = []
             for b in range(list_ref.shape[0]):
                 hit = list_ref[b, 0] == block
@@ -124,14 +135,14 @@
 def near_score_kernel(scale, pos_ref, list_ref, *refs):
     allow_rows(pos_ref, list_ref, refs[-1])
     n = len(NEAR)
-    rows, cents, exps = refs[:n], refs[n : n + SIDE], refs[n + SIDE : -1]
+    rows, cents, exps = refs[:n], refs[n], refs[n + 1 : -1]
     score(scale, NEAR, rows, cents, exps, refs[-1])
 
 
 def far_score_kernel(scale, *refs):
     n = len(FAR)
-    rows, cents, before_ref = refs[:n], refs[n : n + SIDE], refs[n + SIDE]
-    exps, stat_ref = refs[n + SIDE + 1 : -1], refs[-1]
+    rows, cents, before_ref = refs[:n], refs[n], refs[n + 1]
+    exps, stat_ref = refs[n + 2 : -1], refs[-1]
     stat_ref[...] = before_ref[...]
     score(scale, FAR, rows, cents, exps, stat_ref)
 
@@ -144,12 +155,12 @@
 def score(scale, pieces, rows, cents, exps, stat_ref):
     width = rows[0].shape[1]
     for j in range(SIDE):
-        half_norm = read_tail(cents[j], width)
+        half_norm = read_tail(cents.at[j], width)
         for i, (t, half) in enumerate(pieces):
             line = SIDE * SIDE + 2 * SIDE * t + j
             lanes = lanes_of(half, rows[i])
             dots = lax.dot_general(
-                cents[j][:, :width],
+                cents[j, :, :width],
                 rows[i][...],
                 (((1,), (1,)), ((), ())),
                 preferred_element_type=jnp.float32,
@@ -157,7 +168,7 @@
             logits = (dots - half_norm) * scale
             peak = jnp.max(logits, axis=0, keepdims=True)
             exp_values = jnp.exp(logits - peak)
-            exps[i * SIDE + j][...] = exp_values
+            exps[i][j] = exp_values
             stat_ref[line : line + 1, lanes] = peak
             stat_ref[line + SIDE : line + SIDE + 1, lanes] = jnp.sum(
                 exp_values, axis=0, keepdims=True
@@ -212,8 +223,8 @@
 def weighted(j, scale_ref, exps, rows):
     total, lanes = None, None
     for i, (t, half) in enumerate(NEAR + FAR):
-        line = t * SIDE + j
-        weights = exps[i * SIDE + j][...] * scale_ref[line : line + 1, lanes_of(half, rows[i])]
+        factor = scale_ref[pl.ds(t * SIDE + j, 1), lanes_of(half, rows[i])]
+        weights = exps[i][j] * factor
         for start in range(0, weights.shape[1], PAD):
             piece = weights[:, start : start + PAD]
             lanes = piece if lanes is None else lanes + piece
@@ -224,19 +235,18 @@
     return total, jnp.sum(lanes, axis=1, keepdims=True)
 
 
-def sums_kernel(scale_ref, *refs):
+def sums_kernel(pos_ref, scale_ref, *refs):
     n_rows = len(NEAR) + len(FAR)
-    exps, rows = refs[: n_rows * SIDE], refs[n_rows * SIDE : n_rows * (SIDE + 1)]
-    outs = refs[n_rows * (SIDE + 1) :]
+    exps, rows, outs = refs[:n_rows], refs[n_rows : 2 * n_rows], refs[2 * n_rows :]
     width = rows[0].shape[1]
-    for j in range(SIDE - 1, -1, -1):
-        total, counts = weighted(j, scale_ref, exps, rows)
-        if j == 0:
+    for i in range(SIDE - 1, -1, -1):
+        total, counts = weighted(pos_ref[0] ^ SHIFTS[i], scale_ref, exps, rows)
+        if i == 0:
             outs[0][...] = total
             outs[SIDE][...] = jnp.broadcast_to(counts, outs[SIDE].shape)
         else:
-            outs[j][:, :width] = total.astype(jnp.bfloat16)
-            outs[j][:, width:] = tail_lanes(counts)
+            outs[i][:, :width] = total.astype(jnp.bfloat16)
+            outs[i][:, width:] = tail_lanes(counts)
 
 
 def final_kernel(total_ref, count_ref, a_ref, b_ref, c_ref, old_ref, out_ref):
@@ -267,6 +277,10 @@
     return lax.ppermute(value, AXES, pairs)
 
 
+def line_swap(value, groups):
+    return lax.all_to_all(value, AXES, 0, 0, axis_index_groups=groups, tiled=True)
+
+
 def step(embeddings, centroids, candidates):
     planes = lax.axis_size("dp") // CORES
     core = lax.axis_index("dp") % CORES
@@ -278,8 +292,9 @@
     f32, bf16 = jnp.float32, jnp.bfloat16
     shape = jax.ShapeDtypeStruct
 
-    packed = call(pack_kernel, shape((BLK, width + PAD), bf16), 1, 8, nbytes=2 << 20)(centroids)
-    cents = [packed] + [bulk(packed, cent_pairs(planes, SHIFTS[t])) for t in range(1, SIDE)]
+    block_shape = shape((SIDE, BLK, width + PAD), bf16)
+    packed = call(pack_kernel, block_shape, 1, 8, nbytes=4 << 20)(centroids)
+    cents = line_swap(packed, cent_lines(planes))
     half = row_len // 2
     halves = pl.pallas_call(
         split_kernel,
@@ -307,25 +322,25 @@
     stat_shape = shape((SIDE * SIDE + 2 * SIDE * SIDE, row_len), f32)
 
     def exp_shapes(values):
-        return [shape((BLK, value.shape[0]), f32) for value in values for _ in range(SIDE)]
+        return [shape((SIDE, BLK, value.shape[0]), f32) for value in values]
 
     *near_exps, near_stats = call(
         functools.partial(near_score_kernel, factor),
         exp_shapes(near) + [stat_shape],
-        2 + len(near) + SIDE,
+        2 + len(near) + 1,
         16,
         flops=3 * pair_flops,
         nbytes=14 << 20,
         smem=2,
-    )(pos, candidates, *near, *cents)
+    )(pos, candidates, *near, cents)
     *far_exps, own_stats = call(
         functools.partial(far_score_kernel, factor),
         exp_shapes(far) + [stat_shape],
-        len(far) + SIDE + 1,
+        len(far) + 2,
         12,
         flops=pair_flops,
         nbytes=6 << 20,
-    )(*far, *cents, near_stats)
+    )(*far, cents, near_stats)
     exps = near_exps + far_exps
     all_stats = lax.all_gather(own_stats, AXES, axis_index_groups=row_lines(planes))
     n_cover = planes * CORES * SIDE
@@ -343,11 +358,12 @@
         [shape((BLK, width), f32)]
         + [shape((BLK, width + PAD), bf16)] * (SIDE - 1)
         + [shape((BLK, PAD), f32)],
-        1 + len(exps) + len(rows),
+        2 + len(exps) + len(rows),
         24,
         flops=SIDE * pair_flops,
         nbytes=16 << 20,
-    )(scale, *exps, *rows)
+        smem=1,
+    )(cent_pos.reshape(1).astype(jnp.int32), scale, *exps, *rows)
     line_sum, total = lax.optimization_barrier((line_sum, total))
     cover_sums = lax.all_to_all(
         line_sum, AXES, 0, 0, tiled=True, axis_index_groups=line_covers(planes)

time: 121 us -> 124 us (1.025)
  waiting for transfers between devices: 18.9 us -> 29.1 us
  starting transfers between devices: 61.1 us -> 57 us
  local copies, waits for them, and re-layouts: 5.1 us -> 1.86 us
    ppermute x12 -> x9, waiting for transfers between devices: 7.04 us -> 17.3 us  [bulk(): return lax.ppermute(value, AXES, pairs)]
    ppermute x12 -> x9, starting transfers between devices: 35.9 us -> 26.6 us  [bulk(): return lax.ppermute(value, AXES, pairs)]
    all_to_all x0 -> x1, starting transfers between devices: none -> 4.96 us  [line_swap(): lax.all_to_all(value, AXES, 0, 0, axis_index_groups=groups, tiled=True)]
    unnamed x16 -> x10, local copies, waits for them, and re-layouts: 5.1 us -> 1.86 us
    pallas_call x1, Pallas kernels: 0.18 us -> 1.64 us  [step(): packed = call(pack_kernel, block_shape, 1, 8, nbytes=4 << 20)(centroids)]
  transfers between devices with their start and end apart: 13 -> 11, of which waited for: 5 -> 5; matrix products, arithmetic and copies ran while one was open for 0% -> 0% of each run, Pallas kernels for 7% -> 8%
where the time goes in v3:
time: 124 us; the launch traced here: 123 us
  starting transfers between devices  57 us (46%)
  waiting for transfers between devices  29.1 us (23%)
  Pallas kernels  22.3 us (18%)
  blocking collectives  9.63 us (8%)
  between operations  2.59 us (2%)
  local copies, waits for them, and re-layouts  1.86 us (2%)
    ppermute x9, starting transfers between devices, bulk(): return lax.ppermute(value, AXES, pairs)  26.6 us
    all_to_all x1, starting transfers between devices, step(): lax.all_to_all(line_sum, AXES, 0, 0, tiled=True, axis_index_groups=line_c...  25.5 us
    ppermute x9, waiting for transfers between devices, bulk(): return lax.ppermute(value, AXES, pairs)  17.3 us
    all_to_all x1, waiting for transfers between devices, step(): lax.all_to_all(line_sum, AXES, 0, 0, tiled=True, axis_index_groups=line_c...  11.8 us
    all_gather x1, blocking collectives, step(): lax.all_gather(own_stats, AXES, axis_index_groups=row_lines(planes))  9.63 us
    pallas_call x1, Pallas kernels, step(): call(sums_kernel, [shape((BLK, width), f32)] + [shape((BLK, width + PAD),...  7.67 us
    pallas_call x1, Pallas kernels, step(): call(functools.partial(near_score_kernel, factor), exp_shapes(near) + [st...  6.05 us
    all_to_all x1, starting transfers between devices, line_swap(): lax.all_to_all(value, AXES, 0, 0, axis_index_groups=groups, tiled=True)  4.96 us
  transfers between devices with their start and end apart: 11, of which 5 were waited for; matrix products, arithmetic and copies ran while one was open for 0% of the time, Pallas kernels for 8%

profile of v3, /device:TPU:1, one launch (start us, length us, event | category | flops | bytes accessed | tf_op | source)
XLA Modules:
  0.0 123.2 jit_solution(3574179679744622434)
XLA Ops:
  0.6 1.2 copy-done
  1.9 1.6 %shard_map.58 = bf16[4,256,1152]{2,1,0:T(8,128)(2,1)} custom-call(f32[256,1024]{1,0:T(8,128)S(1)} %copy-done), custom_call_target="tpu_custom_call" | custom-call | bytes 4194304 | tf_op jit(solution)/shard_map/pallas_call | solution.py:296
  3.5 5.0 %all-to-all-start = ((bf16[4,256,1152]{2,1,0:T(8,128)(2,1)}), bf16[4,256,1152]{2,1,0:T(8,128)(2,1)S(1)}, u32[]{:S(2)}, u32[]{:S(2)}) async-start(bf16[4,256,1152]{2,1,0:T(8,128)(2,1)} %shard_map.58), calls=%async_computation | async-start | bytes 4718592 | tf_op jit(solution)/shard_map/all_to_all | solution.py:281
  8.5 1.1 split.1
  9.5 4.6 %collective-permute-start.3 = (bf16[256,1024]{1,0:T(8,128)(2,1)}, bf16[256,1024]{1,0:T(8,128)(2,1)}, u32[]{:S(2)}, u32[]{:S(2)}) collective-permute-start(bf16[256,1024]{1,0:T(8,128)(2,1)} %get-tuple-element.26), channel_id=1, source_target_pairs={{12,0},{13,1},{14,2},{15,3},{8,4},{9,5},{10,6},{11,7},{4,8},{5,9},... | collective-permute-start | bytes 1572872 | tf_op jit(solution)/shard_map/ppermute | solution.py:277
  14.2 1.9 %collective-permute-start.2 = (bf16[256,1024]{1,0:T(8,128)(2,1)}, bf16[256,1024]{1,0:T(8,128)(2,1)}, u32[]{:S(2)}, u32[]{:S(2)}) collective-permute-start(bf16[256,1024]{1,0:T(8,128)(2,1)} %get-tuple-element.27), channel_id=1, source_target_pairs={{4,0},{5,1},{6,2},{7,3},{0,4},{1,5},{2,6},{3,7},{12,8},{13,9},{14,... | collective-permute-start | bytes 1572872 | tf_op jit(solution)/shard_map/ppermute | solution.py:277
  16.1 10.0 %collective-permute-done.3.refs_2_.refs_9_ = bf16[256,1024]{1,0:T(8,128)(2,1)} collective-permute-done((bf16[256,1024]{1,0:T(8,128)(2,1)}, bf16[256,1024]{1,0:T(8,128)(2,1)}, u32[]{:S(2)}, u32[]{:S(2)}) %collective-permute-start.3) | collective-permute-done | bytes 524320 | tf_op jit(solution)/shard_map/ppermute | solution.py:277
  26.1 1.9 %collective-permute-start.4 = (bf16[256,1024]{1,0:T(8,128)(2,1)}, bf16[256,1024]{1,0:T(8,128)(2,1)}, u32[]{:S(2)}, u32[]{:S(2)}) collective-permute-start(bf16[256,1024]{1,0:T(8,128)(2,1)} %collective-permute-done.3.refs_2_.refs_9_), channel_id=1, source_target_pairs={{4,0},{5,1},{6,2},{7,3},{0,4},{1,5},{2,6},{3,7},{12,8},{13,9},{14,... | collective-permute-start | bytes 1572872 | tf_op jit(solution)/shard_map/ppermute | solution.py:277
  28.0 2.3 %collective-permute-done.2.refs_1_.refs_8_ = bf16[256,1024]{1,0:T(8,128)(2,1)} collective-permute-done((bf16[256,1024]{1,0:T(8,128)(2,1)}, bf16[256,1024]{1,0:T(8,128)(2,1)}, u32[]{:S(2)}, u32[]{:S(2)}) %collective-permute-start.2) | collective-permute-done | bytes 524320 | tf_op jit(solution)/shard_map/ppermute | solution.py:277
  30.3 3.0 %collective-permute-start.5 = (bf16[256,1024]{1,0:T(8,128)(2,1)}, bf16[256,1024]{1,0:T(8,128)(2,1)}, u32[]{:S(2)}, u32[]{:S(2)}) collective-permute-start(bf16[256,1024]{1,0:T(8,128)(2,1)} %collective-permute-done.2.refs_1_.refs_8_), channel_id=1, source_target_pairs={{12,0},{13,1},{14,2},{15,3},{8,4},{9,5},{10,6},{11,7},{4,8},{5,9},... | collective-permute-start | bytes 1572872 | tf_op jit(solution)/shard_map/ppermute | solution.py:277
  33.4 2.8 %collective-permute-start = (bf16[256,1024]{1,0:T(8,128)(2,1)}, bf16[256,1024]{1,0:T(8,128)(2,1)}, u32[]{:S(2)}, u32[]{:S(2)}) collective-permute-start(bf16[256,1024]{1,0:T(8,128)(2,1)} %get-tuple-element.26), channel_id=1, source_target_pairs={{4,0},{5,1},{6,2},{7,3},{0,4},{1,5},{2,6},{3,7},{12,8},{13,9},{14,... | collective-permute-start | bytes 1572872 | tf_op jit(solution)/shard_map/ppermute | solution.py:277
  36.1 2.6 %collective-permute-start.1 = (bf16[256,1024]{1,0:T(8,128)(2,1)}, bf16[256,1024]{1,0:T(8,128)(2,1)}, u32[]{:S(2)}, u32[]{:S(2)}) collective-permute-start(bf16[256,1024]{1,0:T(8,128)(2,1)} %get-tuple-element.27), channel_id=1, source_target_pairs={{12,0},{13,1},{14,2},{15,3},{8,4},{9,5},{10,6},{11,7},{4,8},{5,9},... | collective-permute-start | bytes 1572872 | tf_op jit(solution)/shard_map/ppermute | solution.py:277
  38.9 2.5 %collective-permute-done.4.refs_3_.refs_10_ = bf16[256,1024]{1,0:T(8,128)(2,1)} collective-permute-done((bf16[256,1024]{1,0:T(8,128)(2,1)}, bf16[256,1024]{1,0:T(8,128)(2,1)}, u32[]{:S(2)}, u32[]{:S(2)}) %collective-permute-start.4) | collective-permute-done | bytes 524320 | tf_op jit(solution)/shard_map/ppermute | solution.py:277
  41.4 2.4 %collective-permute-done.5.refs_4_.refs_11_ = bf16[256,1024]{1,0:T(8,128)(2,1)} collective-permute-done((bf16[256,1024]{1,0:T(8,128)(2,1)}, bf16[256,1024]{1,0:T(8,128)(2,1)}, u32[]{:S(2)}, u32[]{:S(2)}) %collective-permute-start.5) | collective-permute-done | bytes 524320 | tf_op jit(solution)/shard_map/ppermute | solution.py:277
  43.9 6.0 %shard_map.59 = (f32[4,256,512]{2,1,0:T(8,128)S(1)}, f32[4,256,256]{2,1,0:T(8,128)S(1)}, f32[4,256,256]{2,1,0:T(8,128)S(1)}, f32[4,256,256]{2,1,0:T(8,128)S(1)},...) custom-call(s32[3]{0:T(128)S(1)} %pad_add_fusion.pos_ref, s32[2,8]{1,0:T(2,128)S(1)} %copy-done.4, ...), custom_call_target="tpu_custom_call" | custom-call | flops 3221225472 | bytes 14680064 | tf_op jit(solution)/shard_map/pallas_call | solution.py:327
  49.9 2.9 %shard_map.60 = (f32[4,256,256]{2,1,0:T(8,128)S(1)}, f32[4,256,256]{2,1,0:T(8,128)S(1)}, f32[48,512]{1,0:T(8,128)S(1)}) custom-call(bf16[256,1024]{1,0:T(8,128)(2,1)} %collective-permute-done.refs_0_.refs_12_, bf16[256,1024]{1,0:T(8,128)(2,1)} %collective-permute-done.1.refs_1_.refs_13_, bf16[4,256,1152]{2,1,0:T(8,128)(2,1)S(1)} %all-to-all-done.refs_5_.refs_2_, ...), custom_call_target="tpu_custom_call" | custom-call | flops 1073741824 | bytes 6291456 | tf_op jit(solution)/shard_map/pallas_call | solution.py:336
  52.8 9.6 %all-gather = f32[192,512]{1,0:T(8,128)S(1)} all-gather(f32[48,512]{1,0:T(8,128)S(1)} %get-tuple-element.29.own_ref), channel_id=2, replica_groups={{0,4,8,12},{1,5,9,13},{2,6,10,14},{3,7,11,15},{16,17,18,19},{20,21,22,2..., dimensions={0}, use_global_device_ids=true | all-gather | bytes 491520 | tf_op jit(solution)/shard_map/all_gather | solution.py:345
  63.8 7.7 %shard_map.62 = (f32[256,1024]{1,0:T(8,128)S(1)}, bf16[256,1152]{1,0:T(8,128)(2,1)}, bf16[256,1152]{1,0:T(8,128)(2,1)}, bf16[256,1152]{1,0:T(8,128)(2,1)}, f32[256,128]{1,0:T(8,128)S(1)}) custom-call(s32[1]{0:T(128)} %bitcast.2.pos_ref, f32[16,512]{1,0:T(8,128)S(1)} %get-tuple-element.31.scale_ref, f32[4,256,512]{2,1,0:T(8,128)S(1)} %get-tuple-element.32.refs_0_, ...), custom_call_target="tpu_custom_call" | custom-call | flops 4294967296 | bytes 16777216 | tf_op jit(solution)/shard_map/pallas_call | solution.py:356
  71.5 5.0 %collective-permute-start.6 = (bf16[256,1152]{1,0:T(8,128)(2,1)}, bf16[256,1152]{1,0:T(8,128)(2,1)S(1)}, u32[]{:S(2)}, u32[]{:S(2)}) collective-permute-start(bf16[256,1152]{1,0:T(8,128)(2,1)} %get-tuple-element.42), channel_id=1, source_target_pairs={{2,0},{3,1},{0,2},{1,3},{6,4},{7,5},{4,6},{5,7},{10,8},{11,9},{8,1... | collective-permute-start | bytes 1769480 | tf_op jit(solution)/shard_map/ppermute | solution.py:277
  76.5 2.8 %collective-permute-start.7 = (bf16[256,1152]{1,0:T(8,128)(2,1)}, bf16[256,1152]{1,0:T(8,128)(2,1)S(1)}, u32[]{:S(2)}, u32[]{:S(2)}) collective-permute-start(bf16[256,1152]{1,0:T(8,128)(2,1)} %get-tuple-element.43), channel_id=1, source_target_pairs={{3,0},{2,1},{1,2},{0,3},{7,4},{6,5},{5,6},{4,7},{11,8},{10,9},{9,1... | collective-permute-start | bytes 1769480 | tf_op jit(solution)/shard_map/ppermute | solution.py:277
  79.3 1.9 %collective-permute-start.8 = (bf16[256,1152]{1,0:T(8,128)(2,1)}, bf16[256,1152]{1,0:T(8,128)(2,1)}, u32[]{:S(2)}, u32[]{:S(2)}) collective-permute-start(bf16[256,1152]{1,0:T(8,128)(2,1)} %get-tuple-element.44), channel_id=1, source_target_pairs={{1,0},{0,1},{3,2},{2,3},{5,4},{4,5},{7,6},{6,7},{9,8},{8,9},{11,10... | collective-permute-start | bytes 1769480 | tf_op jit(solution)/shard_map/ppermute | solution.py:277
  81.2 25.5 %all-to-all-start.1 = ((f32[128,1,128]{2,1,0:T(1,128)}), f32[128,1,128]{2,1,0:T(1,128)S(1)}, u32[]{:S(2)}, u32[]{:S(2)}) async-start(f32[128,1,128]{2,1,0:T(1,128)} %bitcast.10), calls=%async_computation.1 | async-start | bytes 131072 | tf_op jit(solution)/shard_map/all_to_all | solution.py:368
  106.7 2.3 %final.1 = f32[256,1024]{1,0:T(8,128)} custom-call(f32[256,1024]{1,0:T(8,128)S(1)} %get-tuple-element.40.total_ref, f32[256,128]{1,0:T(8,128)S(1)} %get-tuple-element.41.count_ref, bf16[256,1152]{1,0:T(8,128)(2,1)S(1)} %collective-permute-done.6.a_ref, bf16[256,1152]{1,0:T(8,128)(2,1)S(1)} %collective-permute-done.7.b_ref, ...), custom_call_target="tpu_custom_call" | custom-call | bytes 5242880 | tf_op jit(solution)/shard_map/final/pallas_call | solution.py:374
  109.0 11.8 %all-to-all-done.1 = f32[128,1,128]{2,1,0:T(1,128)S(1)} async-done(((f32[128,1,128]{2,1,0:T(1,128)}), f32[128,1,128]{2,1,0:T(1,128)S(1)}, u32[]{:S(2)}, u32[]{:S(2)}) %all-to-all-start.1) | async-done | bytes 65568 | tf_op jit(solution)/shard_map/all_to_all | solution.py:368
  (18 shorter events, 2.1 us)
Async XLA Ops:
  0.6 1.2 copy-start
  3.5 5.0 %copy-start.2 = (bf16[512,1024]{1,0:T(8,128)(2,1)S(1)}, bf16[512,1024]{1,0:T(8,128)(2,1)}, u32[]{:S(2)}) copy-start(bf16[512,1024]{1,0:T(8,128)(2,1)} %refs_7_.1) | copy-start | bytes 3145732
  3.5 40.4 %copy-start.4 = (s32[2,8]{1,0:T(2,128)S(1)}, s32[2,8]{1,0:T(2,128)}, u32[]{:S(2)}) copy-start(s32[2,8]{1,0:T(2,128)} %list_ref.1) | copy-start | bytes 196
  3.5 40.4 %all-to-all-start = ((bf16[4,256,1152]{2,1,0:T(8,128)(2,1)}), bf16[4,256,1152]{2,1,0:T(8,128)(2,1)S(1)}, u32[]{:S(2)}, u32[]{:S(2)}) async-start(bf16[4,256,1152]{2,1,0:T(8,128)(2,1)} %shard_map.58), calls=%async_computation | async-start | bytes 4718592 | tf_op jit(solution)/shard_map/all_to_all | solution.py:281
  9.5 16.6 %collective-permute-start.3 = (bf16[256,1024]{1,0:T(8,128)(2,1)}, bf16[256,1024]{1,0:T(8,128)(2,1)}, u32[]{:S(2)}, u32[]{:S(2)}) collective-permute-start(bf16[256,1024]{1,0:T(8,128)(2,1)} %get-tuple-element.26), channel_id=1, source_target_pairs={{12,0},{13,1},{14,2},{15,3},{8,4},{9,5},{10,6},{11,7},{4,8},{5,9},... | collective-permute-start | bytes 1572872 | tf_op jit(solution)/shard_map/ppermute | solution.py:277
  14.2 16.2 %collective-permute-start.2 = (bf16[256,1024]{1,0:T(8,128)(2,1)}, bf16[256,1024]{1,0:T(8,128)(2,1)}, u32[]{:S(2)}, u32[]{:S(2)}) collective-permute-start(bf16[256,1024]{1,0:T(8,128)(2,1)} %get-tuple-element.27), channel_id=1, source_target_pairs={{4,0},{5,1},{6,2},{7,3},{0,4},{1,5},{2,6},{3,7},{12,8},{13,9},{14,... | collective-permute-start | bytes 1572872 | tf_op jit(solution)/shard_map/ppermute | solution.py:277
  26.1 15.3 %collective-permute-start.4 = (bf16[256,1024]{1,0:T(8,128)(2,1)}, bf16[256,1024]{1,0:T(8,128)(2,1)}, u32[]{:S(2)}, u32[]{:S(2)}) collective-permute-start(bf16[256,1024]{1,0:T(8,128)(2,1)} %collective-permute-done.3.refs_2_.refs_9_), channel_id=1, source_target_pairs={{4,0},{5,1},{6,2},{7,3},{0,4},{1,5},{2,6},{3,7},{12,8},{13,9},{14,... | collective-permute-start | bytes 1572872 | tf_op jit(solution)/shard_map/ppermute | solution.py:277
  30.3 13.5 %collective-permute-start.5 = (bf16[256,1024]{1,0:T(8,128)(2,1)}, bf16[256,1024]{1,0:T(8,128)(2,1)}, u32[]{:S(2)}, u32[]{:S(2)}) collective-permute-start(bf16[256,1024]{1,0:T(8,128)(2,1)} %collective-permute-done.2.refs_1_.refs_8_), channel_id=1, source_target_pairs={{12,0},{13,1},{14,2},{15,3},{8,4},{9,5},{10,6},{11,7},{4,8},{5,9},... | collective-permute-start | bytes 1572872 | tf_op jit(solution)/shard_map/ppermute | solution.py:277
  33.4 16.5 %collective-permute-start = (bf16[256,1024]{1,0:T(8,128)(2,1)}, bf16[256,1024]{1,0:T(8,128)(2,1)}, u32[]{:S(2)}, u32[]{:S(2)}) collective-permute-start(bf16[256,1024]{1,0:T(8,128)(2,1)} %get-tuple-element.26), channel_id=1, source_target_pairs={{4,0},{5,1},{6,2},{7,3},{0,4},{1,5},{2,6},{3,7},{12,8},{13,9},{14,... | collective-permute-start | bytes 1572872 | tf_op jit(solution)/shard_map/ppermute | solution.py:277
  36.1 13.8 %collective-permute-start.1 = (bf16[256,1024]{1,0:T(8,128)(2,1)}, bf16[256,1024]{1,0:T(8,128)(2,1)}, u32[]{:S(2)}, u32[]{:S(2)}) collective-permute-start(bf16[256,1024]{1,0:T(8,128)(2,1)} %get-tuple-element.27), channel_id=1, source_target_pairs={{12,0},{13,1},{14,2},{15,3},{8,4},{9,5},{10,6},{11,7},{4,8},{5,9},... | collective-permute-start | bytes 1572872 | tf_op jit(solution)/shard_map/ppermute | solution.py:277
  63.2 0.6 copy-start.3
  63.8 42.9 %copy-start.1 = (f32[256,1024]{1,0:T(8,128)S(1)}, f32[256,1024]{1,0:T(8,128)}, u32[]{:S(2)}) copy-start(f32[256,1024]{1,0:T(8,128)} %old_ref.1) | copy-start | bytes 3145732
  71.5 35.2 %collective-permute-start.6 = (bf16[256,1152]{1,0:T(8,128)(2,1)}, bf16[256,1152]{1,0:T(8,128)(2,1)S(1)}, u32[]{:S(2)}, u32[]{:S(2)}) collective-permute-start(bf16[256,1152]{1,0:T(8,128)(2,1)} %get-tuple-element.42), channel_id=1, source_target_pairs={{2,0},{3,1},{0,2},{1,3},{6,4},{7,5},{4,6},{5,7},{10,8},{11,9},{8,1... | collective-permute-start | bytes 1769480 | tf_op jit(solution)/shard_map/ppermute | solution.py:277
  76.5 30.2 %collective-permute-start.7 = (bf16[256,1152]{1,0:T(8,128)(2,1)}, bf16[256,1152]{1,0:T(8,128)(2,1)S(1)}, u32[]{:S(2)}, u32[]{:S(2)}) collective-permute-start(bf16[256,1152]{1,0:T(8,128)(2,1)} %get-tuple-element.43), channel_id=1, source_target_pairs={{3,0},{2,1},{1,2},{0,3},{7,4},{6,5},{5,6},{4,7},{11,8},{10,9},{9,1... | collective-permute-start | bytes 1769480 | tf_op jit(solution)/shard_map/ppermute | solution.py:277
  79.3 27.5 %collective-permute-start.8 = (bf16[256,1152]{1,0:T(8,128)(2,1)}, bf16[256,1152]{1,0:T(8,128)(2,1)}, u32[]{:S(2)}, u32[]{:S(2)}) collective-permute-start(bf16[256,1152]{1,0:T(8,128)(2,1)} %get-tuple-element.44), channel_id=1, source_target_pairs={{1,0},{0,1},{3,2},{2,3},{5,4},{4,5},{7,6},{6,7},{9,8},{8,9},{11,10... | collective-permute-start | bytes 1769480 | tf_op jit(solution)/shard_map/ppermute | solution.py:277
  81.2 39.6 %all-to-all-start.1 = ((f32[128,1,128]{2,1,0:T(1,128)}), f32[128,1,128]{2,1,0:T(1,128)S(1)}, u32[]{:S(2)}, u32[]{:S(2)}) async-start(f32[128,1,128]{2,1,0:T(1,128)} %bitcast.10), calls=%async_computation.1 | async-start | bytes 131072 | tf_op jit(solution)/shard_map/all_to_all | solution.py:368

commit v4 on v2

--- a/solution.py
+++ b/solution.py
@@ -164,7 +164,7 @@
             )
 
 
-def norm_kernel(pos_ref, all_ref, own_ref, scale_ref, log_ref, sum_ref):
+def norm_factors(pos_ref, all_ref, own_ref, scale_ref, log_ref, sum_ref):
     me = pos_ref[0]
     allow_base = 2 * SIDE
 
@@ -224,10 +224,11 @@
     return total, jnp.sum(lanes, axis=1, keepdims=True)
 
 
-def sums_kernel(scale_ref, *refs):
+def sums_kernel(pos_ref, all_ref, own_ref, *refs):
     n_rows = len(NEAR) + len(FAR)
     exps, rows = refs[: n_rows * SIDE], refs[n_rows * SIDE : n_rows * (SIDE + 1)]
-    outs = refs[n_rows * (SIDE + 1) :]
+    *outs, log_ref, sum_ref, scale_ref = refs[n_rows * (SIDE + 1) :]
+    norm_factors(pos_ref, all_ref, own_ref, scale_ref, log_ref, sum_ref)
     width = rows[0].shape[1]
     for j in range(SIDE - 1, -1, -1):
         total, counts = weighted(j, scale_ref, exps, rows)
@@ -249,7 +250,7 @@
     out_ref[...] = total / counts
 
 
-def call(kernel, outs, n_in, limit, flops=0, nbytes=0, smem=0):
+def call(kernel, outs, n_in, limit, flops=0, nbytes=0, smem=0, scratch=()):
     vmem = pl.BlockSpec(memory_space=pltpu.VMEM)
     scalar = pl.BlockSpec(memory_space=pltpu.SMEM)
     in_specs = [scalar] * smem + [vmem] * (n_in - smem)
@@ -258,6 +259,7 @@
         out_shape=outs,
         in_specs=in_specs,
         out_specs=jax.tree.map(lambda _: vmem, outs),
+        scratch_shapes=scratch,
         cost_estimate=pl.CostEstimate(flops=flops, bytes_accessed=nbytes, transcendentals=0),
         compiler_params=pltpu.CompilerParams(vmem_limit_bytes=limit << 20),
     )
@@ -285,7 +287,7 @@
         split_kernel,
         name="split",
         out_shape=[shape((half, width), bf16)] * 2,
-        in_specs=[pl.BlockSpec(memory_space=pl.ANY)],
+        in_specs=[pl.BlockSpec(memory_space=pltpu.HBM)],
         out_specs=[pl.BlockSpec(memory_space=pltpu.VMEM)] * 2,
         scratch_shapes=[pltpu.SemaphoreType.DMA((2,))],
         cost_estimate=pl.CostEstimate(flops=0, bytes_accessed=2 << 20, transcendentals=0),
@@ -329,25 +331,18 @@
     exps = near_exps + far_exps
     all_stats = lax.all_gather(own_stats, AXES, axis_index_groups=row_lines(planes))
     n_cover = planes * CORES * SIDE
-    scale, log_rows, line_sum = call(
-        norm_kernel,
-        [shape((SIDE * SIDE, row_len), f32), shape((1, row_len), f32), shape((n_cover, PAD), f32)],
-        3,
-        4,
-        nbytes=1 << 20,
-        smem=1,
-    )(row_pos.reshape(1).astype(jnp.int32), all_stats, own_stats)
-
-    total, *sent, counts = call(
+    total, *sent, counts, log_rows, line_sum = call(
         sums_kernel,
         [shape((BLK, width), f32)]
         + [shape((BLK, width + PAD), bf16)] * (SIDE - 1)
-        + [shape((BLK, PAD), f32)],
-        1 + len(exps) + len(rows),
+        + [shape((BLK, PAD), f32), shape((1, row_len), f32), shape((n_cover, PAD), f32)],
+        3 + len(exps) + len(rows),
         24,
         flops=SIDE * pair_flops,
         nbytes=16 << 20,
-    )(scale, *exps, *rows)
+        smem=1,
+        scratch=[pltpu.VMEM((SIDE * SIDE, row_len), f32)],
+    )(row_pos.reshape(1).astype(jnp.int32), all_stats, own_stats, *exps, *rows)
     line_sum, total = lax.optimization_barrier((line_sum, total))
     cover_sums = lax.all_to_all(
         line_sum, AXES, 0, 0, tiled=True, axis_index_groups=line_covers(planes)

time: 121 us -> 120 us (level)
  no operation moved by 1% of the time
where the time goes in v4:
time: 120 us
  starting transfers between devices  61.1 us (51%)
  Pallas kernels  20.7 us (17%)
  waiting for transfers between devices  19 us (16%)
  blocking collectives  10.5 us (9%)
  local copies, waits for them, and re-layouts  5.11 us (4%)
  between operations  2.65 us (2%)
    ppermute x12, starting transfers between devices, bulk(): return lax.ppermute(value, AXES, pairs)  35.9 us
    all_to_all x1, starting transfers between devices, step(): lax.all_to_all(line_sum, AXES, 0, 0, tiled=True, axis_index_groups=line_c...  25.2 us
    all_to_all x1, waiting for transfers between devices, step(): lax.all_to_all(line_sum, AXES, 0, 0, tiled=True, axis_index_groups=line_c...  11.9 us
    all_gather x1, blocking collectives, step(): lax.all_gather(own_stats, AXES, axis_index_groups=row_lines(planes))  10.5 us
    pallas_call x1, Pallas kernels, step(): call(sums_kernel, [shape((BLK, width), f32)] + [shape((BLK, width + PAD),...  7.75 us
    ppermute x12, waiting for transfers between devices, bulk(): return lax.ppermute(value, AXES, pairs)  7.04 us
    pallas_call x1, Pallas kernels, step(): call(functools.partial(near_score_kernel, factor), exp_shapes(near) + [st...  6.24 us
    unnamed x16, local copies, waits for them, and re-layouts  5.11 us
  transfers between devices with their start and end apart: 13, of which 5 were waited for; matrix products, arithmetic and copies ran while one was open for 0% of the time, Pallas kernels for 7%

profile of v4, /device:TPU:1, one launch (start us, length us, event | category | flops | bytes accessed | tf_op | source)
XLA Modules:
  0.0 119.7 jit_solution(13753927803499332028)
XLA Ops:
  0.7 1.3 %copy-done.1 = bf16[512,1024]{1,0:T(8,128)(2,1)S(1)} copy-done((bf16[512,1024]{1,0:T(8,128)(2,1)S(1)}, bf16[512,1024]{1,0:T(8,128)(2,1)}, u32[]{:S(2)}) %copy-start.1) | copy-done | bytes 1048600
  2.0 1.1 split.1
  3.1 5.6 %collective-permute-start.6 = (bf16[256,1024]{1,0:T(8,128)(2,1)}, bf16[256,1024]{1,0:T(8,128)(2,1)}, u32[]{:S(2)}, u32[]{:S(2)}) collective-permute-start(bf16[256,1024]{1,0:T(8,128)(2,1)} %get-tuple-element.46), channel_id=1, source_target_pairs={{12,0},{13,1},{14,2},{15,3},{8,4},{9,5},{10,6},{11,7},{4,8},{5,9},... | collective-permute-start | bytes 1572872 | tf_op jit(solution)/shard_map/ppermute | solution.py:269
  8.7 1.9 %collective-permute-start.5 = (bf16[256,1024]{1,0:T(8,128)(2,1)}, bf16[256,1024]{1,0:T(8,128)(2,1)}, u32[]{:S(2)}, u32[]{:S(2)}) collective-permute-start(bf16[256,1024]{1,0:T(8,128)(2,1)} %get-tuple-element.47), channel_id=1, source_target_pairs={{4,0},{5,1},{6,2},{7,3},{0,4},{1,5},{2,6},{3,7},{12,8},{13,9},{14,... | collective-permute-start | bytes 1572872 | tf_op jit(solution)/shard_map/ppermute | solution.py:269
  10.8 4.7 %collective-permute-start.4 = (bf16[256,1152]{1,0:T(8,128)(2,1)S(1)}, bf16[256,1152]{1,0:T(8,128)(2,1)S(1)}, u32[]{:S(2)}, u32[]{:S(2)}) collective-permute-start(bf16[256,1152]{1,0:T(8,128)(2,1)S(1)} %shard_map.58.refs_5_.refs_2_), channel_id=1, source_target_pairs={{2,0},{3,1},{0,2},{1,3},{6,4},{7,5},{4,6},{5,7},{10,8},{11,9},{8,1... | collective-permute-start | bytes 1769480 | tf_op jit(solution)/shard_map/ppermute | solution.py:269
  15.5 2.8 %collective-permute-start.3 = (bf16[256,1152]{1,0:T(8,128)(2,1)S(1)}, bf16[256,1152]{1,0:T(8,128)(2,1)S(1)}, u32[]{:S(2)}, u32[]{:S(2)}) collective-permute-start(bf16[256,1152]{1,0:T(8,128)(2,1)S(1)} %shard_map.58.refs_5_.refs_2_), channel_id=1, source_target_pairs={{3,0},{2,1},{1,2},{0,3},{7,4},{6,5},{5,6},{4,7},{11,8},{10,9},{9,1... | collective-permute-start | bytes 1769480 | tf_op jit(solution)/shard_map/ppermute | solution.py:269
  18.2 1.9 %collective-permute-start.2 = (bf16[256,1152]{1,0:T(8,128)(2,1)S(1)}, bf16[256,1152]{1,0:T(8,128)(2,1)}, u32[]{:S(2)}, u32[]{:S(2)}) collective-permute-start(bf16[256,1152]{1,0:T(8,128)(2,1)S(1)} %shard_map.58.refs_5_.refs_2_), channel_id=1, source_target_pairs={{1,0},{0,1},{3,2},{2,3},{5,4},{4,5},{7,6},{6,7},{9,8},{8,9},{11,10... | collective-permute-start | bytes 1769480 | tf_op jit(solution)/shard_map/ppermute | solution.py:269
  20.2 3.4 %collective-permute-start.7 = (bf16[256,1024]{1,0:T(8,128)(2,1)}, bf16[256,1024]{1,0:T(8,128)(2,1)}, u32[]{:S(2)}, u32[]{:S(2)}) collective-permute-start(bf16[256,1024]{1,0:T(8,128)(2,1)} %collective-permute-done.6.refs_2_.refs_30_), channel_id=1, source_target_pairs={{4,0},{5,1},{6,2},{7,3},{0,4},{1,5},{2,6},{3,7},{12,8},{13,9},{14,... | collective-permute-start | bytes 1572872 | tf_op jit(solution)/shard_map/ppermute | solution.py:269
  23.6 1.9 %collective-permute-start.8 = (bf16[256,1024]{1,0:T(8,128)(2,1)}, bf16[256,1024]{1,0:T(8,128)(2,1)}, u32[]{:S(2)}, u32[]{:S(2)}) collective-permute-start(bf16[256,1024]{1,0:T(8,128)(2,1)} %collective-permute-done.5.refs_1_.refs_29_), channel_id=1, source_target_pairs={{12,0},{13,1},{14,2},{15,3},{8,4},{9,5},{10,6},{11,7},{4,8},{5,9},... | collective-permute-start | bytes 1572872 | tf_op jit(solution)/shard_map/ppermute | solution.py:269
  25.5 1.3 %collective-permute-done.4.refs_8_.refs_5_ = bf16[256,1152]{1,0:T(8,128)(2,1)S(1)} collective-permute-done((bf16[256,1152]{1,0:T(8,128)(2,1)S(1)}, bf16[256,1152]{1,0:T(8,128)(2,1)S(1)}, u32[]{:S(2)}, u32[]{:S(2)}) %collective-permute-start.4) | collective-permute-done | bytes 589856 | tf_op jit(solution)/shard_map/ppermute | solution.py:269
  27.6 2.7 %collective-permute-start = (bf16[256,1024]{1,0:T(8,128)(2,1)}, bf16[256,1024]{1,0:T(8,128)(2,1)}, u32[]{:S(2)}, u32[]{:S(2)}) collective-permute-start(bf16[256,1024]{1,0:T(8,128)(2,1)} %get-tuple-element.46), channel_id=1, source_target_pairs={{4,0},{5,1},{6,2},{7,3},{0,4},{1,5},{2,6},{3,7},{12,8},{13,9},{14,... | collective-permute-start | bytes 1572872 | tf_op jit(solution)/shard_map/ppermute | solution.py:269
  30.4 4.4 %collective-permute-done.3.refs_7_.refs_4_ = bf16[256,1152]{1,0:T(8,128)(2,1)S(1)} collective-permute-done((bf16[256,1152]{1,0:T(8,128)(2,1)S(1)}, bf16[256,1152]{1,0:T(8,128)(2,1)S(1)}, u32[]{:S(2)}, u32[]{:S(2)}) %collective-permute-start.3) | collective-permute-done | bytes 589856 | tf_op jit(solution)/shard_map/ppermute | solution.py:269
  35.6 1.9 %collective-permute-start.1 = (bf16[256,1024]{1,0:T(8,128)(2,1)}, bf16[256,1024]{1,0:T(8,128)(2,1)}, u32[]{:S(2)}, u32[]{:S(2)}) collective-permute-start(bf16[256,1024]{1,0:T(8,128)(2,1)} %get-tuple-element.47), channel_id=1, source_target_pairs={{12,0},{13,1},{14,2},{15,3},{8,4},{9,5},{10,6},{11,7},{4,8},{5,9},... | collective-permute-start | bytes 1572872 | tf_op jit(solution)/shard_map/ppermute | solution.py:269
  37.7 1.1 collective-permute-done.8.refs_4_.refs_32_
  40.9 6.2 %shard_map.59 = (f32[256,512]{1,0:T(8,128)S(1)}, f32[256,512]{1,0:T(8,128)S(1)}, f32[256,512]{1,0:T(8,128)S(1)}, f32[256,512]{1,0:T(8,128)S(1)}, f32[256,256]{1,...) custom-call(s32[3]{0:T(128)S(1)} %pad_add_fusion.pos_ref, ...), custom_call_target="tpu_custom_call" | custom-call | flops 3221225472 | bytes 14680064 | tf_op jit(solution)/shard_map/pallas_call | solution.py:314
  47.3 3.1 %shard_map.60 = (f32[256,256]{1,0:T(8,128)S(1)}, f32[256,256]{1,0:T(8,128)S(1)}, f32[256,256]{1,0:T(8,128)S(1)}, f32[256,256]{1,0:T(8,128)S(1)}, f32[256,256]{1,...) custom-call(bf16[256,1024]{1,0:T(8,128)(2,1)} %collective-permute-do, ...), custom_call_target="tpu_custom_call" | custom-call | flops 1073741824 | bytes 6291456 | tf_op jit(solution)/shard_map/pallas_call | solution.py:323
  50.4 10.5 %all-gather = f32[192,512]{1,0:T(8,128)S(1)} all-gather(f32[48,512]{1,0:T(8,128)S(1)} %get-tuple-element.49.own_ref), channel_id=2, replica_groups={{0,4,8,12},{1,5,9,13},{2,6,10,14},{3,7,11,15},{16,17,18,19},{20,21,22,2..., dimensions={0}, use_global_device_ids=true | all-gather | bytes 491520 | tf_op jit(solution)/shard_map/all_gather | solution.py:332
  60.9 7.7 %shard_map.61 = (f32[256,1024]{1,0:T(8,128)S(1)}, bf16[256,1152]{1,0:T(8,128)(2,1)}, bf16[256,1152]{1,0:T(8,128)(2,1)}, bf16[256,1152]{1,0:T(8,128)(2,1)}, f32[2...) custom-call(s32[1]{0:T(128)} %bitcast.pos_ref, f32[4,48,512]{2,1,0:T(8,128)S(1)} %bitcast.9, ...), custom_call_target="tpu_custom_call" | custom-call | flops 4294967296 | bytes 16777216 | tf_op jit(solution)/shard_map/pallas_call | solution.py:334
  68.7 5.2 %collective-permute-start.9 = (bf16[256,1152]{1,0:T(8,128)(2,1)}, bf16[256,1152]{1,0:T(8,128)(2,1)S(1)}, u32[]{:S(2)}, u32[]{:S(2)}) collective-permute-start(bf16[256,1152]{1,0:T(8,128)(2,1)} %get-tuple-element.82), channel_id=1, source_target_pairs={{2,0},{3,1},{0,2},{1,3},{6,4},{7,5},{4,6},{5,7},{10,8},{11,9},{8,1... | collective-permute-start | bytes 1769480 | tf_op jit(solution)/shard_map/ppermute | solution.py:269
  73.9 1.9 %collective-permute-start.10 = (bf16[256,1152]{1,0:T(8,128)(2,1)}, bf16[256,1152]{1,0:T(8,128)(2,1)S(1)}, u32[]{:S(2)}, u32[]{:S(2)}) collective-permute-start(bf16[256,1152]{1,0:T(8,128)(2,1)} %get-tuple-element.83), channel_id=1, source_target_pairs={{3,0},{2,1},{1,2},{0,3},{7,4},{6,5},{5,6},{4,7},{11,8},{10,9},{9,1... | collective-permute-start | bytes 1769480 | tf_op jit(solution)/shard_map/ppermute | solution.py:269
  75.8 1.9 %collective-permute-start.11 = (bf16[256,1152]{1,0:T(8,128)(2,1)}, bf16[256,1152]{1,0:T(8,128)(2,1)}, u32[]{:S(2)}, u32[]{:S(2)}) collective-permute-start(bf16[256,1152]{1,0:T(8,128)(2,1)} %get-tuple-element.84), channel_id=1, source_target_pairs={{1,0},{0,1},{3,2},{2,3},{5,4},{4,5},{7,6},{6,7},{9,8},{8,9},{11,10... | collective-permute-start | bytes 1769480 | tf_op jit(solution)/shard_map/ppermute | solution.py:269
  77.8 25.2 %all-to-all-start = ((f32[128,1,128]{2,1,0:T(1,128)}), f32[128,1,128]{2,1,0:T(1,128)S(1)}, u32[]{:S(2)}, u32[]{:S(2)}) async-start(f32[128,1,128]{2,1,0:T(1,128)} %bitcast.5), calls=%async_computation | async-start | bytes 131072 | tf_op jit(solution)/shard_map/all_to_all | solution.py:347
  103.0 2.3 %final.1 = f32[256,1024]{1,0:T(8,128)} custom-call(f32[256,1024]{1,0:T(8,128)S(1)} %get-tuple-element.80.total_ref, f32[256,128]{1,0:T(8,128)S(1)} %get-tuple-element.81.count_ref, bf16[256,1152]{1,0:T(8,128)(2,1)S(1)} %collective-permute-done.9.a_ref, bf16[256,1152]{1,0:T(8,128)(2,1)S(1)} %collective-permute-done.10.b_ref, ...), custom_call_target="tpu_custom_call" | custom-call | bytes 5242880 | tf_op jit(solution)/shard_map/final/pallas_call | solution.py:353
  105.4 11.9 %all-to-all-done = f32[128,1,128]{2,1,0:T(1,128)S(1)} async-done(((f32[128,1,128]{2,1,0:T(1,128)}), f32[128,1,128]{2,1,0:T(1,128)S(1)}, u32[]{:S(2)}, u32[]{:S(2)}) %all-to-all-start) | async-done | bytes 65568 | tf_op jit(solution)/shard_map/all_to_all | solution.py:347
  (27 shorter events, 4.9 us)
Async XLA Ops:
  0.6 10.0 %copy-start = (f32[256,1024]{1,0:T(8,128)S(1)}, f32[256,1024]{1,0:T(8,128)}, u32[]{:S(2)}) copy-start(f32[256,1024]{1,0:T(8,128)} %old_ref.1) | copy-start | bytes 3145732
  0.6 1.3 %copy-start.1 = (bf16[512,1024]{1,0:T(8,128)(2,1)S(1)}, bf16[512,1024]{1,0:T(8,128)(2,1)}, u32[]{:S(2)}) copy-start(bf16[512,1024]{1,0:T(8,128)(2,1)} %refs_28_.1) | copy-start | bytes 3145732
  3.1 35.7 %copy-start.2 = (bf16[512,1024]{1,0:T(8,128)(2,1)S(1)}, bf16[512,1024]{1,0:T(8,128)(2,1)}, u32[]{:S(2)}) copy-start(bf16[512,1024]{1,0:T(8,128)(2,1)} %refs_28_.1) | copy-start | bytes 3145732
  3.1 17.1 %collective-permute-start.6 = (bf16[256,1024]{1,0:T(8,128)(2,1)}, bf16[256,1024]{1,0:T(8,128)(2,1)}, u32[]{:S(2)}, u32[]{:S(2)}) collective-permute-start(bf16[256,1024]{1,0:T(8,128)(2,1)} %get-tuple-element.46), channel_id=1, source_target_pairs={{12,0},{13,1},{14,2},{15,3},{8,4},{9,5},{10,6},{11,7},{4,8},{5,9},... | collective-permute-start | bytes 1572872 | tf_op jit(solution)/shard_map/ppermute | solution.py:269
  8.7 14.9 %collective-permute-start.5 = (bf16[256,1024]{1,0:T(8,128)(2,1)}, bf16[256,1024]{1,0:T(8,128)(2,1)}, u32[]{:S(2)}, u32[]{:S(2)}) collective-permute-start(bf16[256,1024]{1,0:T(8,128)(2,1)} %get-tuple-element.47), channel_id=1, source_target_pairs={{4,0},{5,1},{6,2},{7,3},{0,4},{1,5},{2,6},{3,7},{12,8},{13,9},{14,... | collective-permute-start | bytes 1572872 | tf_op jit(solution)/shard_map/ppermute | solution.py:269
  10.8 16.0 %collective-permute-start.4 = (bf16[256,1152]{1,0:T(8,128)(2,1)S(1)}, bf16[256,1152]{1,0:T(8,128)(2,1)S(1)}, u32[]{:S(2)}, u32[]{:S(2)}) collective-permute-start(bf16[256,1152]{1,0:T(8,128)(2,1)S(1)} %shard_map.58.refs_5_.refs_2_), channel_id=1, source_target_pairs={{2,0},{3,1},{0,2},{1,3},{6,4},{7,5},{4,6},{5,7},{10,8},{11,9},{8,1... | collective-permute-start | bytes 1769480 | tf_op jit(solution)/shard_map/ppermute | solution.py:269
  15.5 19.3 %collective-permute-start.3 = (bf16[256,1152]{1,0:T(8,128)(2,1)S(1)}, bf16[256,1152]{1,0:T(8,128)(2,1)S(1)}, u32[]{:S(2)}, u32[]{:S(2)}) collective-permute-start(bf16[256,1152]{1,0:T(8,128)(2,1)S(1)} %shard_map.58.refs_5_.refs_2_), channel_id=1, source_target_pairs={{3,0},{2,1},{1,2},{0,3},{7,4},{6,5},{5,6},{4,7},{11,8},{10,9},{9,1... | collective-permute-start | bytes 1769480 | tf_op jit(solution)/shard_map/ppermute | solution.py:269
  18.2 19.4 %collective-permute-start.2 = (bf16[256,1152]{1,0:T(8,128)(2,1)S(1)}, bf16[256,1152]{1,0:T(8,128)(2,1)}, u32[]{:S(2)}, u32[]{:S(2)}) collective-permute-start(bf16[256,1152]{1,0:T(8,128)(2,1)S(1)} %shard_map.58.refs_5_.refs_2_), channel_id=1, source_target_pairs={{1,0},{0,1},{3,2},{2,3},{5,4},{4,5},{7,6},{6,7},{9,8},{8,9},{11,10... | collective-permute-start | bytes 1769480 | tf_op jit(solution)/shard_map/ppermute | solution.py:269
  20.2 17.5 %collective-permute-start.7 = (bf16[256,1024]{1,0:T(8,128)(2,1)}, bf16[256,1024]{1,0:T(8,128)(2,1)}, u32[]{:S(2)}, u32[]{:S(2)}) collective-permute-start(bf16[256,1024]{1,0:T(8,128)(2,1)} %collective-permute-done.6.refs_2_.refs_30_), channel_id=1, source_target_pairs={{4,0},{5,1},{6,2},{7,3},{0,4},{1,5},{2,6},{3,7},{12,8},{13,9},{14,... | collective-permute-start | bytes 1572872 | tf_op jit(solution)/shard_map/ppermute | solution.py:269
  23.6 15.2 %collective-permute-start.8 = (bf16[256,1024]{1,0:T(8,128)(2,1)}, bf16[256,1024]{1,0:T(8,128)(2,1)}, u32[]{:S(2)}, u32[]{:S(2)}) collective-permute-start(bf16[256,1024]{1,0:T(8,128)(2,1)} %collective-permute-done.5.refs_1_.refs_29_), channel_id=1, source_target_pairs={{12,0},{13,1},{14,2},{15,3},{8,4},{9,5},{10,6},{11,7},{4,8},{5,9},... | collective-permute-start | bytes 1572872 | tf_op jit(solution)/shard_map/ppermute | solution.py:269
  26.8 0.8 copy-start.3
  27.6 19.5 %collective-permute-start = (bf16[256,1024]{1,0:T(8,128)(2,1)}, bf16[256,1024]{1,0:T(8,128)(2,1)}, u32[]{:S(2)}, u32[]{:S(2)}) collective-permute-start(bf16[256,1024]{1,0:T(8,128)(2,1)} %get-tuple-element.46), channel_id=1, source_target_pairs={{4,0},{5,1},{6,2},{7,3},{0,4},{1,5},{2,6},{3,7},{12,8},{13,9},{14,... | collective-permute-start | bytes 1572872 | tf_op jit(solution)/shard_map/ppermute | solution.py:269
  34.8 0.8 copy-start.5
  35.6 11.7 %collective-permute-start.1 = (bf16[256,1024]{1,0:T(8,128)(2,1)}, bf16[256,1024]{1,0:T(8,128)(2,1)}, u32[]{:S(2)}, u32[]{:S(2)}) collective-permute-start(bf16[256,1024]{1,0:T(8,128)(2,1)} %get-tuple-element.47), channel_id=1, source_target_pairs={{12,0},{13,1},{14,2},{15,3},{8,4},{9,5},{10,6},{11,7},{4,8},{5,9},... | collective-permute-start | bytes 1572872 | tf_op jit(solution)/shard_map/ppermute | solution.py:269
  37.6 1.2 copy-start.7
  38.7 1.1 copy-start.4
  39.8 1.1 copy-start.6
  68.7 34.4 %collective-permute-start.9 = (bf16[256,1152]{1,0:T(8,128)(2,1)}, bf16[256,1152]{1,0:T(8,128)(2,1)S(1)}, u32[]{:S(2)}, u32[]{:S(2)}) collective-permute-start(bf16[256,1152]{1,0:T(8,128)(2,1)} %get-tuple-element.82), channel_id=1, source_target_pairs={{2,0},{3,1},{0,2},{1,3},{6,4},{7,5},{4,6},{5,7},{10,8},{11,9},{8,1... | collective-permute-start | bytes 1769480 | tf_op jit(solution)/shard_map/ppermute | solution.py:269
  73.9 29.1 %collective-permute-start.10 = (bf16[256,1152]{1,0:T(8,128)(2,1)}, bf16[256,1152]{1,0:T(8,128)(2,1)S(1)}, u32[]{:S(2)}, u32[]{:S(2)}) collective-permute-start(bf16[256,1152]{1,0:T(8,128)(2,1)} %get-tuple-element.83), channel_id=1, source_target_pairs={{3,0},{2,1},{1,2},{0,3},{7,4},{6,5},{5,6},{4,7},{11,8},{10,9},{9,1... | collective-permute-start | bytes 1769480 | tf_op jit(solution)/shard_map/ppermute | solution.py:269
  75.8 27.2 %collective-permute-start.11 = (bf16[256,1152]{1,0:T(8,128)(2,1)}, bf16[256,1152]{1,0:T(8,128)(2,1)}, u32[]{:S(2)}, u32[]{:S(2)}) collective-permute-start(bf16[256,1152]{1,0:T(8,128)(2,1)} %get-tuple-element.84), channel_id=1, source_target_pairs={{1,0},{0,1},{3,2},{2,3},{5,4},{4,5},{7,6},{6,7},{9,8},{8,9},{11,10... | collective-permute-start | bytes 1769480 | tf_op jit(solution)/shard_map/ppermute | solution.py:269
  77.8 39.5 %all-to-all-start = ((f32[128,1,128]{2,1,0:T(1,128)}), f32[128,1,128]{2,1,0:T(1,128)S(1)}, u32[]{:S(2)}, u32[]{:S(2)}) async-start(f32[128,1,128]{2,1,0:T(1,128)} %bitcast.5), calls=%async_computation | async-start | bytes 131072 | tf_op jit(solution)/shard_map/all_to_all | solution.py:347
